TPU v7x, 32 devices: a whole 2x2x4 slice. The times are simulated.
32 devices in a mesh: seq: 8 (over z, y), head: 4 (over x, core).
Axes of the slice: x: 2, y: 2, z: 4, core: 2. Of those that a mesh axis runs over, the one named last changes fastest.
Arguments:
- query_rows: bfloat16 [16384, 2048], P('seq', 'head'), may hold values from -6 to 6
- key_rows: bfloat16 [16384, 2048], P('seq', 'head'), may hold values from -6 to 6
- value_rows: bfloat16 [16384, 2048], P('seq', 'head'), may hold values from -6 to 6
- out_cotangent: bfloat16 [16384, 2048], P('seq', 'head'), may hold values from -6 to 6
- norm_gain: float32 [2048], P('head'), may hold values from 0.5 to 1.5
- decay_rate: float32 [16], P('head'), may hold values from 1.2207031e-05 to 0.0333333333
- document_lengths: int32 [32], replicated, may hold values from 1 to 8192, 16384 in all
- group_home: int32 [64], P('seq'), may hold values from 0 to 63, as said below
Outputs:
- query_grad: bfloat16 [16384, 2048], P('seq', 'head')
- key_grad: bfloat16 [16384, 2048], P('seq', 'head')
- value_grad: bfloat16 [16384, 2048], P('seq', 'head')
Inputs may be any that keep to these rules, and one draw needn't show every extreme that they name: document_lengths sum to 16384; the longest holds exactly half of them. group_home is a permutation of the 64 sequence groups; the groups stored on one device along seq hold exactly one group of each device's aligned block of sequence groups.
All inputs are finite; a program needn't handle non-finite values.
Results may differ from a plain program's by a relative error of at most 0.0095.
Values may be sent and summed in bfloat16 or wider, within the bound.
No kernel may reach another device: no remote copies, remote signals or barrier semaphores. Data moves between devices by JAX's collectives and lax.ppermute only.
A program may use at most 128 MiB of HBM per device.

v0:
```python
import functools

import jax
import jax.numpy as jnp
from jax import lax
from jax.experimental import pallas as pl
from jax.experimental.pallas import tpu as pltpu
from jax.sharding import PartitionSpec as P


HEAD_SIZE = 128
LANES = 128
EPSILON = 1e-06
UNROLL = {"summary": 4, "local": 4, "output": 8, "cotangent": 8, "inner_grads": 4, "outer_grads": 2}
TAIL = 16
ALONE = 58
LIMIT = 16
F32 = jnp.float32
BF16 = jnp.bfloat16


def dot(a, b, ca, cb):
    return lax.dot_general(a, b, (((ca,), (cb,)), ((), ())), preferred_element_type=F32)


def head_cols(h):
    return slice(h * HEAD_SIZE, (h + 1) * HEAD_SIZE)


def token_index(span):
    return lax.broadcasted_iota(jnp.int32, (span, LANES), 0)


def key_side(rate, span):
    return jnp.exp(-rate * (span - 1.0 - token_index(span).astype(F32)))


def query_side(rate, span):
    return jnp.exp(-rate * (token_index(span).astype(F32) + 1.0))


def fill_decay(decay, rate_ref, base, span):
    j = lax.broadcasted_iota(jnp.int32, (span, span), 0)
    l = lax.broadcasted_iota(jnp.int32, (span, span), 1)
    spread = (j - l).astype(F32)
    for h in range(decay.shape[0]):
        falling = jnp.exp(-rate_ref[base + h] * jnp.maximum(spread, 0.0))
        decay[h] = jnp.where(spread >= 0.0, falling, 0.0)


def row_to_cols(row, width):
    cols = jnp.transpose(jnp.broadcast_to(row, (LANES, row.shape[1])))
    return jnp.concatenate([cols] * (width // LANES), axis=1) if width > LANES else cols


def cols_to_row(cols):
    return jnp.sum(jnp.transpose(cols), axis=0, keepdims=True)


def fill_tables(len_ref, first_ref, last_ref, span):
    spans = first_ref.shape[0] - 1
    far = jnp.int32(spans * span)

    def reset(c, carry):
        first_ref[c] = far
        last_ref[c] = 0
        return carry

    def note(d, end):
        end = end + len_ref[d]
        c = lax.shift_right_logical(end, span.bit_length() - 1) if span & (span - 1) == 0 else end // span
        inside = end - c * span
        last_ref[c] = inside
        first_ref[c] = jnp.minimum(first_ref[c], inside)
        return end

    lax.fori_loop(0, spans + 1, reset, 0, unroll=8)
    lax.fori_loop(0, len_ref.shape[0], note, jnp.int32(0), unroll=4)
    first_ref[0] = 0


def fill_segments(seg_ref, len_ref, home_ref):
    slots, span = seg_ref.shape
    slot = lax.broadcasted_iota(jnp.int32, (slots, span), 0)
    position = lax.broadcasted_iota(jnp.int32, (slots, span), 1)
    for i in range(slots):
        position += jnp.where(slot == i, home_ref[i] * span, 0)

    def note(d, carry):
        end, segment = carry
        end = end + len_ref[d]
        return end, segment + jnp.where(end <= position, 1.0, 0.0)

    start = (jnp.int32(0), jnp.zeros((slots, span), F32))
    seg_ref[...] = lax.fori_loop(0, len_ref.shape[0], note, start, unroll=4)[1]


def tokens_at(i, span):
    return pl.ds(pl.multiple_of(i * span, span), span)


def rows_at(i, rows):
    return pl.ds(pl.multiple_of(i * rows, rows), rows)


def get_state(ref, i, h, rows):
    chunks = HEAD_SIZE // rows
    return ref[h * chunks : (h + 1) * chunks, rows_at(i, rows), :].reshape(HEAD_SIZE, HEAD_SIZE)


def span_copies(i, span, sources, targets, sem):
    at = tokens_at(i, span)
    return [
        pltpu.make_async_copy(source.at[at], target.at[at], sem.at[a, i])
        for a, (source, target) in enumerate(zip(sources, targets))
    ]


def start_all(copies):
    for copy in copies:
        copy.start()


def wait_all(copies):
    for copy in copies:
        copy.wait()


def each_span(slots, unroll, load, compute, store):
    def turn(g, carry):
        group = [g * unroll + j for j in range(unroll)]
        for i in group:
            wait_all(load(i))
        for i in group:
            compute(i)
        for i in group:
            start_all(store(i))
        return carry

    lax.fori_loop(0, slots // unroll, turn, 0)


def nothing(i):
    return []


def own_index():
    return lax.axis_index("seq")


def group_head(group, chunks):
    head = jnp.bitwise_xor(own_index() // chunks, group)
    return head, pl.ds(pl.multiple_of(head * HEAD_SIZE, HEAD_SIZE), HEAD_SIZE)


def put_group(packed, g, i, rows, value):
    chunks = HEAD_SIZE // rows
    for part in range(chunks):
        packed[g * chunks + part, rows_at(i, rows), :] = value[part * rows : (part + 1) * rows]


def get_group(packed, g, i, rows):
    chunks = HEAD_SIZE // rows
    return packed[g * chunks : (g + 1) * chunks, rows_at(i, rows), :].reshape(HEAD_SIZE, HEAD_SIZE)


def give_groups(packed, blocks, chunks, size):
    turn = own_index() % chunks
    for n, block in enumerate(blocks):
        block[:size] = packed[n // chunks * chunks + jnp.bitwise_xor(turn, n % chunks)]


def take_groups(blocks, packed, chunks):
    turn = own_index() % chunks
    for n, block in enumerate(blocks):
        packed[n // chunks * chunks + jnp.bitwise_xor(turn, n % chunks)] = block[...]


def take_blocks(blocks, packed):
    me = own_index()
    for mask, block in enumerate(blocks):
        packed[jnp.bitwise_xor(me, mask)] = block[...]


def summary_kernel(groups, rows, span, count, lead, *refs):
    if lead:
        len_ref, home_ref, rate_ref, k_hbm, v_hbm = refs[:5]
        blocks, refs = refs[5 : 5 + count], refs[5 + count :]
        first_ref, last_ref, k_ref, v_ref, table, packed, sem = refs
    else:
        last_ref, home_ref, rate_ref, k_hbm, v_hbm = refs[:5]
        blocks, refs = refs[5 : 5 + count], refs[5 + count :]
        k_ref, v_ref, table, packed, sem = refs
    slots = home_ref.shape[0]
    chunks = HEAD_SIZE // rows
    heads = [group_head(p, chunks) for p in groups]
    sources = [ref.at[:, heads[0][1]] if lead else ref for ref in (k_hbm, v_hbm)]
    load = lambda i: span_copies(i, span, sources, (k_ref, v_ref), sem)
    for i in range(slots):
        start_all(load(i))
    if lead:
        fill_tables(len_ref, first_ref, last_ref, span)
    for g, (head, cols) in enumerate(heads):
        table[g] = key_side(rate_ref[head], span)
    tail = jnp.zeros((TAIL, LANES), F32)
    lane = lax.broadcasted_iota(jnp.int32, (TAIL, LANES), 1)
    for i in range(slots):
        tail = jnp.where(lane == i, home_ref[i].astype(F32), tail)
    for block in blocks:
        block[slots * rows :, :] = tail.astype(BF16)

    def body(i):
        at = tokens_at(i, span)
        live = token_index(span) >= last_ref[home_ref[i]]
        for g, (head, cols) in enumerate(heads):
            cols = slice(None) if lead else cols
            side = jnp.where(live, table[g], 0.0)
            weighted = (side * v_ref[at, cols].astype(F32)).astype(BF16)
            put_group(packed, g, i, rows, dot(k_ref[at, cols], weighted, 0, 0).astype(BF16))

    each_span(slots, UNROLL["summary"], load, body, nothing)
    give_groups(packed, blocks, chunks, slots * rows)


def scan_kernel(rows, span, reverse, count, first_ref, order_in, rate_ref, *refs):
    sources, refs = refs[:count], refs[count if reverse else count + 1 :]
    targets, refs = refs[:count], refs[count:]
    if reverse:
        order_ref = order_in
        arrived, states = refs
    else:
        order_ref, arrived, states, homes, home_ref, home_sem = refs
    slots = states.shape[1] // rows
    spans = order_ref.shape[0]
    if not reverse:
        for k, ref in enumerate(sources):
            homes[k : k + 1, :] = ref[slots * rows :, :].astype(F32)[0:1].astype(jnp.int32)
        gather = pltpu.make_async_copy(homes, home_ref, home_sem)
        gather.start()
    for k, ref in enumerate(sources):
        arrived[k] = ref[: slots * rows]
    head = (own_index() * rows) // HEAD_SIZE
    factor = jnp.exp(jnp.full((8, LANES), -rate_ref[head] * span, F32))[0:1]
    if not reverse:
        gather.wait()

        def note(k, carry):
            for i in range(slots):
                order_ref[home_ref[k, i]] = k * slots + i
            return carry

        lax.fori_loop(0, count, note, 0)

    def body(i, state):
        c = spans - 1 - i if reverse else i
        place = order_ref[c]
        block, slot = place // slots, place % slots
        at = rows_at(slot, rows)
        states[block, at, :] = state.astype(BF16)
        carried = jnp.where(first_ref[c] >= span, factor * state, 0.0)
        return carried + arrived[block, at, :].astype(F32)

    lax.fori_loop(0, spans, body, jnp.zeros((rows, LANES), F32), unroll=4)
    for k, ref in enumerate(targets):
        ref[...] = states[k]


def local_kernel(
    heads, span, len_ref, home_ref, rate_ref, q_hbm, u_hbm, k_ref, v_ref,
    out_ref, q_ref, u_ref, seg_ref, decay, sem, u_sem,
):
    slots = home_ref.shape[0]
    load = lambda i: span_copies(i, span, (q_hbm,), (q_ref,), sem)
    later = lambda i: span_copies(i, span, (u_hbm,), (u_ref,), u_sem)
    for i in range(slots):
        start_all(load(i))
    for i in range(slots):
        start_all(later(i))
    fill_segments(seg_ref, len_ref, home_ref)
    fill_decay(decay, rate_ref, 0, span)

    def body(i):
        at = tokens_at(i, span)
        seg = seg_ref[pl.ds(i, 1), :]
        same = row_to_cols(seg, span) == seg
        for h in range(heads):
            cols = head_cols(h)
            scores = dot(q_ref[at, cols], k_ref[at, cols], 1, 1)
            mixing = (scores * jnp.where(same, decay[h], 0.0)).astype(BF16)
            out_ref[at, cols] = dot(mixing, v_ref[at, cols], 1, 0)

    each_span(slots, UNROLL["local"], load, body, nothing)
    for i in range(slots):
        wait_all(later(i))


def output_kernel(
    groups, rows, span, count, again, first_ref, home_ref, rate_ref, gain_ref, q_ref, u_ref, inner_ref, *refs
):
    blocks, refs = refs[:count], refs[count:]
    if again:
        before_ref, refs = refs[0], refs[2:]
    out_ref, sums_ref, prev, table = refs
    slots = home_ref.shape[0]
    chunks = HEAD_SIZE // rows
    heads = [group_head(p, chunks) for p in groups]
    take_groups(blocks, prev, chunks)
    for g, (head, cols) in enumerate(heads):
        table[g] = query_side(rate_ref[head], span)

    def body(i):
        at = tokens_at(i, span)
        live = token_index(span) < first_ref[home_ref[i]]
        squares = jnp.zeros((span, LANES), F32)
        crossed = jnp.zeros((span, LANES), F32)
        for g, (head, cols) in enumerate(heads):
            outer = dot(q_ref[at, cols], get_group(prev, g, i, rows), 1, 0)
            attn = inner_ref[at, cols] + jnp.where(live, table[g], 0.0) * outer
            out_ref[at, cols] = attn
            squares += attn * attn
            crossed += gain_ref[:, cols] * u_ref[at, cols].astype(F32) * attn
        squares, crossed = cols_to_row(squares), cols_to_row(crossed)
        if again:
            squares += before_ref[0, pl.ds(i, 1), :]
            crossed += before_ref[1, pl.ds(i, 1), :]
        sums_ref[0, pl.ds(i, 1), :] = squares
        sums_ref[1, pl.ds(i, 1), :] = crossed

    each_span(slots, UNROLL["output"], nothing, body, nothing)


def cotangent_kernel(
    groups, rows, span, count, again, channels, others, first_ref, home_ref, rate_ref, gain_ref, q_ref, u_ref, attn_ref, *refs
):
    sums, refs = refs[:others], refs[others + again :]
    g_ref, blocks = refs[0], refs[1 : 1 + count]
    table, factors, packed = refs[1 + count :]
    slots = home_ref.shape[0]
    chunks = HEAD_SIZE // rows
    heads = [group_head(p, chunks) for p in groups]
    scaling = 1.0 / jnp.sqrt(sum(ref[0] for ref in sums) / channels + EPSILON)
    pulled = sum(ref[1] for ref in sums) / channels
    factors[0] = scaling
    factors[1] = scaling * scaling * scaling * pulled
    for g, (head, cols) in enumerate(heads):
        table[g] = query_side(rate_ref[head], span)

    def body(i):
        at = tokens_at(i, span)
        direct = row_to_cols(factors[0, pl.ds(i, 1), :], LANES)
        along = row_to_cols(factors[1, pl.ds(i, 1), :], LANES)
        live = token_index(span) < first_ref[home_ref[i]]
        for g, (head, cols) in enumerate(heads):
            grad = direct * gain_ref[:, cols] * u_ref[at, cols].astype(F32)
            grad = (grad - along * attn_ref[at, cols]).astype(BF16)
            g_ref[at, cols] = grad
            weighted = (jnp.where(live, table[g], 0.0) * grad.astype(F32)).astype(BF16)
            put_group(packed, g, i, rows, dot(q_ref[at, cols], weighted, 0, 0).astype(BF16))

    each_span(slots, UNROLL["cotangent"], nothing, body, nothing)
    give_groups(packed, blocks, chunks, slots * rows)


def inner_grads_kernel(
    heads, rows, span, count, half, first_ref, home_ref, rate_ref, seg_ref, q_ref, k_ref, v_ref, g_ref, *refs
):
    blocks, refs = refs[:count], refs[count + half :]
    dq_hbm, dk_ref, dv_ref, dq_ref, prev, decay, table, out_sem = refs
    slots = home_ref.shape[0] // 2
    base = half * slots
    target = dq_hbm.at[pl.ds(base * span, slots * span)]
    store = lambda i: span_copies(i, span, (dq_ref,), (target,), out_sem)
    take_blocks(blocks, prev)
    fill_decay(decay, rate_ref, 0, span)
    for h in range(heads):
        table[h] = query_side(rate_ref[h], span)

    def body(own):
        i = base + own
        at, own = tokens_at(i, span), tokens_at(own, span)
        seg = seg_ref[pl.ds(i, 1), :]
        same = row_to_cols(seg, span) == seg
        live = token_index(span) < first_ref[home_ref[i]]
        for h in range(heads):
            cols = head_cols(h)
            q, k, v, g = q_ref[at, cols], k_ref[at, cols], v_ref[at, cols], g_ref[at, cols]
            mask = jnp.where(same, decay[h], 0.0)
            mixing = (dot(q, k, 1, 1) * mask).astype(BF16)
            score_grad = (dot(g, v, 1, 1) * mask).astype(BF16)
            outer = dot(g, get_state(prev, i, h, rows), 1, 1)
            dq = dot(score_grad, k, 1, 0) + jnp.where(live, table[h], 0.0) * outer
            dq_ref[own, cols] = dq.astype(BF16)
            dk_ref[own, cols] = dot(score_grad, q, 0, 0)
            dv_ref[own, cols] = dot(mixing, g, 0, 0)

    each_span(slots, UNROLL["inner_grads"], nothing, body, store)
    for i in range(slots):
        wait_all(store(i))


def outer_grads_kernel(
    groups, rows, span, count, again, last_ref, home_ref, rate_ref, k_ref, v_ref, dk_0, dv_0, dk_1, dv_1, *refs
):
    blocks, refs = refs[:count], refs[count + 2 * again :]
    dk_hbm, dv_hbm, dk_ref, dv_ref, after_ref, table, out_sem = refs
    slots = home_ref.shape[0]
    chunks = HEAD_SIZE // rows
    heads = [group_head(p, chunks) for p in groups]

    def store(i):
        copies = []
        for g, (head, cols) in enumerate(heads):
            targets = (dk_hbm.at[:, cols], dv_hbm.at[:, cols])
            sources = (dk_ref.at[g], dv_ref.at[g])
            copies += span_copies(i, span, sources, targets, out_sem.at[g])
        return copies

    take_groups(blocks, after_ref, chunks)
    for g, (head, cols) in enumerate(heads):
        table[g] = key_side(rate_ref[head], span)

    def body(half, own):
        dk_in, dv_in = ((dk_0, dv_0), (dk_1, dv_1))[half]
        i = half * (slots // 2) + own
        at, own = tokens_at(i, span), tokens_at(own, span)
        live = token_index(span) >= last_ref[home_ref[i]]
        for g, (head, cols) in enumerate(heads):
            side = jnp.where(live, table[g], 0.0)
            after = get_group(after_ref, g, i, rows)
            dk = dk_in[own, cols] + side * dot(v_ref[at, cols], after, 1, 1)
            dv = dv_in[own, cols] + side * dot(k_ref[at, cols], after, 1, 0)
            dk_ref[g, at, :] = dk.astype(BF16)
            dv_ref[g, at, :] = dv.astype(BF16)

    for half in range(2):
        keep = lambda own, half=half: store(half * (slots // 2) + own)
        each_span(slots // 2, 4 if len(groups) == 1 else UNROLL["outer_grads"], nothing, functools.partial(body, half), keep)
    for i in range(slots):
        wait_all(store(i))


def swap(array, axis, mask):
    if mask == 0:
        return array
    return lax.ppermute(array, axis, [(i, i ^ mask) for i in range(lax.axis_size(axis))])


def exchange(blocks):
    moved = [None] * len(blocks)
    for mask in range(len(blocks) - 1, -1, -1):
        moved[mask] = swap(blocks[mask], "seq", mask)
    return moved


def shards(query, key, value, upstream, norm_gain, decay_rate, document_lengths, group_home):
    devices = lax.axis_size("seq")
    assert devices & (devices - 1) == 0
    tokens, width = query.shape
    heads = width // HEAD_SIZE
    slots = group_home.shape[0]
    span = tokens // slots
    spans = slots * devices
    rows = width // devices
    channels = width * lax.axis_size("head")

    gain = norm_gain.reshape(1, width)

    smem = pl.BlockSpec(memory_space=pltpu.SMEM)
    vmem = pl.BlockSpec(memory_space=pltpu.VMEM)
    hbm = pl.BlockSpec(memory_space=pl.ANY)
    spans_table = jax.ShapeDtypeStruct((spans + 1,), jnp.int32)
    whole = jax.ShapeDtypeStruct((tokens, width), BF16)
    token_bf16 = pltpu.VMEM((tokens, width), BF16)
    token_f32 = pltpu.VMEM((tokens, width), F32)
    table = pltpu.VMEM((heads, span, LANES), F32)
    decay = pltpu.VMEM((heads, span, span), F32)
    states = pltpu.VMEM((devices, slots * rows, LANES), BF16)
    out = [jax.ShapeDtypeStruct(states.shape[1:], BF16)] * devices
    taken = [vmem] * devices
    chunks = devices // heads
    assert heads > 1 and heads & (heads - 1) == 0
    final = heads // 2
    ahead, behind = (heads - 1,), tuple(range(heads - 2, -1, -1))
    early, late = tuple(p for p in range(heads - 1, -1, -1) if p != final), (final,)

    def masks_of(groups):
        return [p * chunks + n for p in groups for n in range(chunks)]

    def pick(blocks, groups):
        return [blocks[mask] for mask in masks_of(groups)]

    def states_of(groups):
        return pltpu.VMEM((len(groups) * chunks, slots * rows, LANES), BF16)

    def table_of(groups):
        return pltpu.VMEM((len(groups), span, LANES), F32)

    def sems(*shape):
        return pltpu.SemaphoreType.DMA(shape)

    def call(kernel, limit, flops, in_specs, out_specs, out_shape, scratch, *static, aliases={}):
        return pl.pallas_call(
            functools.partial(kernel, *static),
            in_specs=in_specs,
            out_specs=out_specs,
            out_shape=out_shape,
            scratch_shapes=scratch,
            input_output_aliases=aliases,
            compiler_params=pltpu.CompilerParams(vmem_limit_bytes=limit << 20),
            cost_estimate=pl.CostEstimate(flops=flops, bytes_accessed=0, transcendentals=0),
        )

    work = 2 * tokens * width * span
    shape = [jax.ShapeDtypeStruct((slots * rows + TAIL, LANES), BF16)]
    count = len(masks_of(ahead))
    *sent, first, last = call(
        summary_kernel, ALONE, work // 8,
        [smem, smem, smem, hbm, hbm],
        [vmem] * count + [smem, smem],
        shape * count + [spans_table, spans_table],
        [pltpu.VMEM((tokens, HEAD_SIZE), BF16)] * 2 + [table_of(ahead), states_of(ahead), sems(2, slots)],
        ahead, rows, span, count, True,
    )(document_lengths, group_home, decay_rate, key, value)
    moving = dict(zip(masks_of(ahead), sent))
    count = len(masks_of(behind))
    *sent, key_v, value_v = call(
        summary_kernel, ALONE, work // 2,
        [smem, smem, smem, hbm, hbm],
        [vmem] * (count + 2),
        shape * count + [token_bf16, token_bf16],
        [table_of(behind), states_of(behind), sems(2, slots)],
        behind, rows, span, count, False,
    )(last, group_home, decay_rate, key, value)
    moving.update(zip(masks_of(behind), sent))
    arrived = exchange(moving)

    inner, query_v, upstream_v, seg = call(
        local_kernel, LIMIT, 2 * work,
        [smem, smem, smem, hbm, hbm, vmem, vmem],
        [vmem, vmem, vmem, vmem],
        [token_f32, token_bf16, token_bf16, pltpu.VMEM((slots, span), F32)],
        [decay, sems(1, slots), sems(1, slots)],
        heads, span,
    )(document_lengths, group_home, decay_rate, query, upstream, key_v, value_v)

    def scan(arrived, order, reverse, *after_it):
        held = [states, states]
        if reverse:
            extra_specs, extra = [], []
        else:
            extra_specs, extra = [smem], [jax.ShapeDtypeStruct((spans,), jnp.int32)]
            table_shape = (devices, LANES)
            held += [pltpu.VMEM(table_shape, jnp.int32), pltpu.SMEM(table_shape, jnp.int32), pltpu.SemaphoreType.DMA]
        return call(
            scan_kernel, LIMIT, work // 8,
            [smem, smem, smem] + taken + [hbm] * len(after_it),
            taken + extra_specs,
            out + extra,
            held,
            rows, span, reverse, devices,
        )(first, order, decay_rate, *arrived, *after_it)

    *moving, order = scan(arrived, group_home, False, seg)
    prev = exchange(moving)

    def outputs(groups, *before):
        count = len(masks_of(groups))
        again = len(before) > 0
        return call(
            output_kernel, LIMIT, work // 4,
            [smem, smem, smem] + [vmem] * (4 + count + len(before)),
            [vmem, vmem],
            [token_f32, jax.ShapeDtypeStruct((2, slots, span), F32)],
            [states_of(groups), table_of(groups)],
            groups, rows, span, count, again,
            aliases={8 + count: 0} if again else {},
        )(first, group_home, decay_rate, gain, query_v, upstream_v, inner, *pick(prev, groups), *before)

    attn, sums = outputs(early)
    attn, sums = outputs(late, sums, attn)
    sums = [swap(sums, "head", mask) for mask in range(lax.axis_size("head") - 1, -1, -1)]

    def cotangents(groups, *before):
        count = len(masks_of(groups))
        others = len(sums)
        return call(
            cotangent_kernel, LIMIT, work // 4,
            [smem, smem, smem] + [vmem] * (4 + others + len(before)),
            [vmem] * (1 + count),
            [token_bf16] + out[:count],
            [table_of(groups), pltpu.VMEM((2, slots, span), F32), states_of(groups)],
            groups, rows, span, count, len(before), channels, others,
            aliases={7 + others: 0} if before else {},
        )(first, group_home, decay_rate, gain, query_v, upstream_v, attn, *sums, *before)

    grad_in, *sent = cotangents(ahead)
    moving = dict(zip(masks_of(ahead), sent))
    grad_in, *sent = cotangents(behind, grad_in)
    moving.update(zip(masks_of(behind), sent))
    arrived = exchange(moving)

    half_f32 = pltpu.VMEM((tokens // 2, width), F32)

    def inner_grads(half, *into):
        return call(
            inner_grads_kernel, LIMIT, 3 * work,
            [smem, smem, smem, vmem, vmem, vmem, vmem, vmem] + taken + [hbm] * half,
            [hbm, vmem, vmem],
            [whole, half_f32, half_f32],
            [pltpu.VMEM((tokens // 2, width), BF16), states, decay, table, sems(1, slots // 2)],
            heads, rows, span, devices, half,
            aliases={8 + devices: 0} if half else {},
        )(first, group_home, decay_rate, seg, query_v, key_v, value_v, grad_in, *prev, *into)

    query_half, *parts = inner_grads(0)
    query_grad, *others = inner_grads(1, query_half)
    after = exchange(scan(arrived, order, True))

    def outer_grads(groups, *before):
        count = len(masks_of(groups))
        part = pltpu.VMEM((len(groups), tokens, HEAD_SIZE), BF16)
        return call(
            outer_grads_kernel, LIMIT, work // 2,
            [smem, smem, smem] + [vmem] * (6 + count) + [hbm] * len(before),
            [hbm, hbm],
            [whole, whole],
            [part, part, states_of(groups), table_of(groups), sems(len(groups), 2, slots)],
            groups, rows, span, count, len(before) > 0,
            aliases={9 + count: 0, 10 + count: 1} if before else {},
        )(last, group_home, decay_rate, key_v, value_v, *parts, *others, *pick(after, groups), *before)

    finals = outer_grads(early)
    key_grad, value_grad = outer_grads(late, *finals)
    return query_grad, key_grad, value_grad


def solution(mesh):
    in_specs = (
        P("seq", "head"),
        P("seq", "head"),
        P("seq", "head"),
        P("seq", "head"),
        P("head"),
        P("head"),
        P(),
        P("seq"),
    )
    out_specs = (P("seq", "head"), P("seq", "head"), P("seq", "head"))

    return jax.shard_map(shards, mesh=mesh, in_specs=in_specs, out_specs=out_specs, check_vma=False)
```

profile of v0, /device:TPU:0, one launch (start us, length us, event | category | flops | bytes accessed | tf_op | source)
XLA Modules:
  0.0 131.4 jit_solution(5362307128646001463)
XLA Ops:
  0.6 3.2 %shard_map.103 = (bf16[528,128]{1,0:T(8,128)(2,1)}, bf16[528,128]{1,0:T(8,128)(2,1)}, s32[65]{0:T(128)}, s32[65]{0:T(128)}) custom-call(s32[32]{0:T(128)} %len_ref.1, s32[8]{0:T(128)} %home_ref.17, f32[4]{0:T(128)} %rate_ref.21, bf16[2048,512]{1,0:T(8,128)(2,1)} %refs_3_.3, bf16[2048,512]{1,0:T(8,128)(2,1)} %refs_4_.3), custom_call_target="tpu_custom_call" | custom-call | flops 67108864 | tf_op jit(solution)/shard_map/pallas_call | solution.py:516
  3.8 5.1 %collective-permute-start.5 = (bf16[528,128]{1,0:T(8,128)(2,1)}, bf16[528,128]{1,0:T(8,128)(2,1)S(1)}, u32[]{:S(2)}, u32[]{:S(2)}) collective-permute-start(bf16[528,128]{1,0:T(8,128)(2,1)} %get-tuple-element.74), channel_id=1, source_target_pairs={{0,24},{4,28},{8,16},{12,20},{16,8},{20,12},{24,0},{28,4},{1,25},{... | collective-permute-start | bytes 405512 | tf_op jit(solution)/shard_map/ppermute | solution.py:445
  9.0 1.2 collective-permute-start.6
  10.2 4.5 %shard_map.104 = (bf16[528,128]{1,0:T(8,128)(2,1)}, bf16[528,128]{1,0:T(8,128)(2,1)}, bf16[528,128]{1,0:T(8,128)(2,1)}, bf16[528,128]{1,0:T(8,128)(2,1)}, bf16[5...) custom-call(s32[65]{0:T(128)} %get-tuple-element.61.refs_0_.last_ref, ...), custom_call_target="tpu_custom_call" | custom-call | flops 268435456 | tf_op jit(solution)/shard_map/pallas_call | solution.py:526
  15.1 3.1 %collective-permute-start.2 = (bf16[528,128]{1,0:T(8,128)(2,1)}, bf16[528,128]{1,0:T(8,128)(2,1)S(1)}, u32[]{:S(2)}, u32[]{:S(2)}) collective-permute-start(bf16[528,128]{1,0:T(8,128)(2,1)} %get-tuple-element.71), channel_id=1, source_target_pairs={{0,12},{4,8},{8,4},{12,0},{16,28},{20,24},{24,20},{28,16},{1,13},{... | collective-permute-start | bytes 405512 | tf_op jit(solution)/shard_map/ppermute | solution.py:445
  18.3 2.2 %collective-permute-start.3 = (bf16[528,128]{1,0:T(8,128)(2,1)}, bf16[528,128]{1,0:T(8,128)(2,1)S(1)}, u32[]{:S(2)}, u32[]{:S(2)}) collective-permute-start(bf16[528,128]{1,0:T(8,128)(2,1)} %get-tuple-element.72), channel_id=1, source_target_pairs={{0,16},{4,20},{8,24},{12,28},{16,0},{20,4},{24,8},{28,12},{1,17},{... | collective-permute-start | bytes 405512 | tf_op jit(solution)/shard_map/ppermute | solution.py:445
  20.5 2.9 %collective-permute-start.4 = (bf16[528,128]{1,0:T(8,128)(2,1)}, bf16[528,128]{1,0:T(8,128)(2,1)S(1)}, u32[]{:S(2)}, u32[]{:S(2)}) collective-permute-start(bf16[528,128]{1,0:T(8,128)(2,1)} %get-tuple-element.73), channel_id=1, source_target_pairs={{0,20},{4,16},{8,28},{12,24},{16,4},{20,0},{24,12},{28,8},{1,21},{... | collective-permute-start | bytes 405512 | tf_op jit(solution)/shard_map/ppermute | solution.py:445
  23.3 1.6 %copy-done = bf16[2048,512]{1,0:T(8,128)(2,1)S(1)} copy-done((bf16[2048,512]{1,0:T(8,128)(2,1)S(1)}, bf16[2048,512]{1,0:T(8,128)(2,1)}, u32[]{:S(2)}) %copy-start) | copy-done | bytes 2097176
  24.9 1.6 %copy-done.1 = bf16[2048,512]{1,0:T(8,128)(2,1)S(1)} copy-done((bf16[2048,512]{1,0:T(8,128)(2,1)S(1)}, bf16[2048,512]{1,0:T(8,128)(2,1)}, u32[]{:S(2)}) %copy-start.1) | copy-done | bytes 2097176
  26.5 4.3 %shard_map.105 = (f32[2048,512]{1,0:T(8,128)S(1)}, bf16[2048,512]{1,0:T(8,128)(2,1)S(1)}, bf16[2048,512]{1,0:T(8,128)(2,1)S(1)}, f32[8,256]{1,0:T(8,128)S(1)}) custom-call(s32[32]{0:T(128)S(1)} %copy-done.8, s32[8]{0:T(128)S(1)} %copy-done.4, f32[4]{0:T(128)S(1)} %copy-done.3, bf16[2048,512]{1,0:T(8,128)(2,1)S(1)} %copy-done, ...), custom_call_target="tpu_custom_call" | custom-call | flops 1073741824 | tf_op jit(solution)/shard_map/pallas_call | solution.py:537
  30.9 0.5 collective-permute-done.3.refs_4_
  31.4 2.0 %collective-permute-done.4.refs_5_ = bf16[528,128]{1,0:T(8,128)(2,1)S(1)} collective-permute-done((bf16[528,128]{1,0:T(8,128)(2,1)}, bf16[528,128]{1,0:T(8,128)(2,1)S(1)}, u32[]{:S(2)}, u32[]{:S(2)}) %collective-permute-start.4) | collective-permute-done | bytes 135200 | tf_op jit(solution)/shard_map/ppermute | solution.py:445
  33.3 2.5 %shard_map.106 = (bf16[512,128]{1,0:T(8,128)(2,1)S(1)}, bf16[512,128]{1,0:T(8,128)(2,1)S(1)}, bf16[512,128]{1,0:T(8,128)(2,1)S(1)}, bf16[512,128]{1,0:T(8,128)(2...) custom-call(s32[65]{0:T(128)S(1)} %copy-done.5, ...), custom_call_target="tpu_custom_call" | custom-call | flops 67108864 | tf_op jit(solution)/shard_map/pallas_call | solution.py:554
  35.8 2.5 %collective-permute-start.9 = (bf16[512,128]{1,0:T(8,128)(2,1)S(1)}, bf16[512,128]{1,0:T(8,128)(2,1)S(1)}, u32[]{:S(2)}, u32[]{:S(2)}) collective-permute-start(bf16[512,128]{1,0:T(8,128)(2,1)S(1)} %get-tuple-element.78), channel_id=1, source_target_pairs={{0,24},{4,28},{8,16},{12,20},{16,8},{20,12},{24,0},{28,4},{1,25},{... | collective-permute-start | bytes 393224 | tf_op jit(solution)/shard_map/ppermute | solution.py:445
  38.3 2.0 %collective-permute-start.10 = (bf16[512,128]{1,0:T(8,128)(2,1)S(1)}, bf16[512,128]{1,0:T(8,128)(2,1)S(1)}, u32[]{:S(2)}, u32[]{:S(2)}) collective-permute-start(bf16[512,128]{1,0:T(8,128)(2,1)S(1)} %get-tuple-element.79), channel_id=1, source_target_pairs={{0,28},{4,24},{8,20},{12,16},{16,12},{20,8},{24,4},{28,0},{1,29},{... | collective-permute-start | bytes 393224 | tf_op jit(solution)/shard_map/ppermute | solution.py:445
  40.4 2.3 %collective-permute-start.12 = (bf16[512,128]{1,0:T(8,128)(2,1)S(1)}, bf16[512,128]{1,0:T(8,128)(2,1)S(1)}, u32[]{:S(2)}, u32[]{:S(2)}) collective-permute-start(bf16[512,128]{1,0:T(8,128)(2,1)S(1)} %get-tuple-element.81), channel_id=1, source_target_pairs={{0,12},{4,8},{8,4},{12,0},{16,28},{20,24},{24,20},{28,16},{1,13},{... | collective-permute-start | bytes 393224 | tf_op jit(solution)/shard_map/ppermute | solution.py:445
  42.6 1.2 collective-permute-start.13
  43.9 1.1 collective-permute-start.7
  45.0 2.4 %collective-permute-done.10.refs_1_.refs_7_ = bf16[512,128]{1,0:T(8,128)(2,1)S(1)} collective-permute-done((bf16[512,128]{1,0:T(8,128)(2,1)S(1)}, bf16[512,128]{1,0:T(8,128)(2,1)S(1)}, u32[]{:S(2)}, u32[]{:S(2)}) %collective-permute-start.10) | collective-permute-done | bytes 131104 | tf_op jit(solution)/shard_map/ppermute | solution.py:445
  47.4 2.2 %collective-permute-start.8 = (bf16[512,128]{1,0:T(8,128)(2,1)S(1)}, bf16[512,128]{1,0:T(8,128)(2,1)S(1)}, u32[]{:S(2)}, u32[]{:S(2)}) collective-permute-start(bf16[512,128]{1,0:T(8,128)(2,1)S(1)} %get-tuple-element.77), channel_id=1, source_target_pairs={{0,20},{4,16},{8,28},{12,24},{16,4},{20,0},{24,12},{28,8},{1,21},{... | collective-permute-start | bytes 393224 | tf_op jit(solution)/shard_map/ppermute | solution.py:445
  49.6 1.9 %collective-permute-done.11.refs_2_ = bf16[512,128]{1,0:T(8,128)(2,1)S(1)} collective-permute-done((bf16[512,128]{1,0:T(8,128)(2,1)S(1)}, bf16[512,128]{1,0:T(8,128)(2,1)S(1)}, u32[]{:S(2)}, u32[]{:S(2)}) %collective-permute-start.11) | collective-permute-done | bytes 131104 | tf_op jit(solution)/shard_map/ppermute | solution.py:445
  51.5 4.2 %collective-permute-done.12.refs_3_ = bf16[512,128]{1,0:T(8,128)(2,1)S(1)} collective-permute-done((bf16[512,128]{1,0:T(8,128)(2,1)S(1)}, bf16[512,128]{1,0:T(8,128)(2,1)S(1)}, u32[]{:S(2)}, u32[]{:S(2)}) %collective-permute-start.12) | collective-permute-done | bytes 131104 | tf_op jit(solution)/shard_map/ppermute | solution.py:445
  55.7 2.5 %shard_map.107 = (f32[2048,512]{1,0:T(8,128)S(1)}, f32[2,8,256]{2,1,0:T(8,128)S(1)}) custom-call(s32[65]{0:T(128)S(1)} %copy-done.5, s32[8]{0:T(128)S(1)} %copy-done.4, f32[4]{0:T(128)S(1)} %copy-done.3, f32[1,512]{1,0:T(1,128)S(1)} %bitcast.1, bf16[2048,512]{1,0:T(8,128)(2,1)S(1)} %get-tuple-element.65.q_ref, ...), custom_call_target="tpu_custom_call" | custom-call | flops 134217728 | tf_op jit(solution)/shard_map/pallas_call | solution.py:569
  58.2 0.7 collective-permute-done.8.refs_1_.refs_5_
  58.9 1.4 %shard_map.108 = (f32[2048,512]{1,0:T(8,128)S(1)}, f32[2,8,256]{2,1,0:T(8,128)S(1)}) custom-call(s32[65]{0:T(128)S(1)} %copy-done.5, s32[8]{0:T(128)S(1)} %copy-done.4, f32[4]{0:T(128)S(1)} %copy-done.3, f32[1,512]{1,0:T(1,128)S(1)} %bitcast.2, bf16[2048,512]{1,0:T(8,128)(2,1)S(1)} %get-tuple-element.65.q_ref, ...), custom_call_target="tpu_custom_call", output_to_operand_aliasing={{0}: (10, {})} | custom-call | flops 134217728 | tf_op jit(solution)/shard_map/pallas_call | solution.py:569
  60.4 1.6 %collective-permute-start.15 = (f32[2,8,256]{2,1,0:T(8,128)S(1)}, f32[2,8,256]{2,1,0:T(8,128)S(1)}, u32[]{:S(2)}, u32[]{:S(2)}) collective-permute-start(f32[2,8,256]{2,1,0:T(8,128)S(1)} %get-tuple-element.87.refs_3_), channel_id=1, source_target_pairs={{0,2},{1,3},{2,0},{3,1},{4,6},{5,7},{6,4},{7,5},{8,10},{9,11},{10,... | collective-permute-start | bytes 49160 | tf_op jit(solution)/shard_map/ppermute | solution.py:445
  62.2 2.0 %collective-permute-done.15.refs_1_ = f32[2,8,256]{2,1,0:T(8,128)S(1)} collective-permute-done((f32[2,8,256]{2,1,0:T(8,128)S(1)}, f32[2,8,256]{2,1,0:T(8,128)S(1)}, u32[]{:S(2)}, u32[]{:S(2)}) %collective-permute-start.15) | collective-permute-done | bytes 16416 | tf_op jit(solution)/shard_map/ppermute | solution.py:445
  64.2 0.9 collective-permute-done.14.refs_0_
  65.1 1.7 %shard_map.109 = (bf16[2048,512]{1,0:T(8,128)(2,1)S(1)}, bf16[512,128]{1,0:T(8,128)(2,1)S(1)}, bf16[512,128]{1,0:T(8,128)(2,1)S(1)}) custom-call(s32[65]{0:T(128)S(1)} %copy-done.5, s32[8]{0:T(128)S(1)} %copy-done.4, f32[4]{0:T(128)S(1)} %copy-done.3, f32[1,512]{1,0:T(1,128)S(1)} %bitcast.3, bf16[2048,512]{1,0:T(8,128)(2,1)S(1)} %get-tuple-element.65.q_ref, ...), custom_call_target="tpu_custom_call" | custom-call | flops 134217728 | tf_op jit(solution)/shard_map/pallas_call | solution.py:586
  66.8 2.6 %shard_map.110 = (bf16[2048,512]{1,0:T(8,128)(2,1)S(1)}, bf16[512,128]{1,0:T(8,128)(2,1)S(1)}, bf16[512,128]{1,0:T(8,128)(2,1)S(1)}, bf16[512,128]{1,0:T(8,128)(...) custom-call(s32[65]{0:T(128)S(1)} %copy-done.5, ...), custom_call_target="tpu_custom_call", output_to_operand_aliasing={{0}: (11, {})} | custom-call | flops 134217728 | tf_op jit(solution)/shard_map/pallas_call | solution.py:586
  69.4 1.4 %collective-permute-start.17 = (bf16[512,128]{1,0:T(8,128)(2,1)S(1)}, bf16[512,128]{1,0:T(8,128)(2,1)S(1)}, u32[]{:S(2)}, u32[]{:S(2)}) collective-permute-start(bf16[512,128]{1,0:T(8,128)(2,1)S(1)} %get-tuple-element.98), channel_id=1, source_target_pairs={{0,4},{4,0},{8,12},{12,8},{16,20},{20,16},{24,28},{28,24},{1,5},{5... | collective-permute-start | bytes 393224 | tf_op jit(solution)/shard_map/ppermute | solution.py:445
  70.8 2.2 %collective-permute-start.19 = (bf16[512,128]{1,0:T(8,128)(2,1)S(1)}, bf16[512,128]{1,0:T(8,128)(2,1)S(1)}, u32[]{:S(2)}, u32[]{:S(2)}) collective-permute-start(bf16[512,128]{1,0:T(8,128)(2,1)S(1)} %get-tuple-element.100), channel_id=1, source_target_pairs={{0,12},{4,8},{8,4},{12,0},{16,28},{20,24},{24,20},{28,16},{1,13},{... | collective-permute-start | bytes 393224 | tf_op jit(solution)/shard_map/ppermute | solution.py:445
  73.4 3.2 %collective-permute-start.21 = (bf16[512,128]{1,0:T(8,128)(2,1)S(1)}, bf16[512,128]{1,0:T(8,128)(2,1)S(1)}, u32[]{:S(2)}, u32[]{:S(2)}) collective-permute-start(bf16[512,128]{1,0:T(8,128)(2,1)S(1)} %get-tuple-element.102), channel_id=1, source_target_pairs={{0,20},{4,16},{8,28},{12,24},{16,4},{20,0},{24,12},{28,8},{1,21},{... | collective-permute-start | bytes 393224 | tf_op jit(solution)/shard_map/ppermute | solution.py:445
  76.6 1.5 %collective-permute-start.22 = (bf16[512,128]{1,0:T(8,128)(2,1)S(1)}, bf16[512,128]{1,0:T(8,128)(2,1)S(1)}, u32[]{:S(2)}, u32[]{:S(2)}) collective-permute-start(bf16[512,128]{1,0:T(8,128)(2,1)S(1)} %get-tuple-element.103), channel_id=1, source_target_pairs={{0,24},{4,28},{8,16},{12,20},{16,8},{20,12},{24,0},{28,4},{1,25},{... | collective-permute-start | bytes 393224 | tf_op jit(solution)/shard_map/ppermute | solution.py:445
  78.1 1.9 %collective-permute-done.18.refs_2_ = bf16[512,128]{1,0:T(8,128)(2,1)S(1)} collective-permute-done((bf16[512,128]{1,0:T(8,128)(2,1)S(1)}, bf16[512,128]{1,0:T(8,128)(2,1)S(1)}, u32[]{:S(2)}, u32[]{:S(2)}) %collective-permute-start.18) | collective-permute-done | bytes 131104 | tf_op jit(solution)/shard_map/ppermute | solution.py:445
  80.0 2.3 %collective-permute-start.23 = (bf16[512,128]{1,0:T(8,128)(2,1)S(1)}, bf16[512,128]{1,0:T(8,128)(2,1)S(1)}, u32[]{:S(2)}, u32[]{:S(2)}) collective-permute-start(bf16[512,128]{1,0:T(8,128)(2,1)S(1)} %get-tuple-element.104), channel_id=1, source_target_pairs={{0,28},{4,24},{8,20},{12,16},{16,12},{20,8},{24,4},{28,0},{1,29},{... | collective-permute-start | bytes 393224 | tf_op jit(solution)/shard_map/ppermute | solution.py:445
  82.4 9.1 %collective-permute-done.20.refs_4_ = bf16[512,128]{1,0:T(8,128)(2,1)S(1)} collective-permute-done((bf16[512,128]{1,0:T(8,128)(2,1)S(1)}, bf16[512,128]{1,0:T(8,128)(2,1)S(1)}, u32[]{:S(2)}, u32[]{:S(2)}) %collective-permute-start.20) | collective-permute-done | bytes 131104 | tf_op jit(solution)/shard_map/ppermute | solution.py:445
  91.5 3.5 %collective-permute-done.21.refs_5_ = bf16[512,128]{1,0:T(8,128)(2,1)S(1)} collective-permute-done((bf16[512,128]{1,0:T(8,128)(2,1)S(1)}, bf16[512,128]{1,0:T(8,128)(2,1)S(1)}, u32[]{:S(2)}, u32[]{:S(2)}) %collective-permute-start.21) | collective-permute-done | bytes 131104 | tf_op jit(solution)/shard_map/ppermute | solution.py:445
  95.0 1.5 %shard_map.113 = (bf16[512,128]{1,0:T(8,128)(2,1)S(1)}, bf16[512,128]{1,0:T(8,128)(2,1)S(1)}, bf16[512,128]{1,0:T(8,128)(2,1)S(1)}, bf16[512,128]{1,0:T(8,128)(2...) custom-call(s32[65]{0:T(128)S(1)} %copy-done.5, ...), custom_call_target="tpu_custom_call" | custom-call | flops 67108864 | tf_op jit(solution)/shard_map/pallas_call | solution.py:554
  96.5 1.5 %collective-permute-start.26 = (bf16[512,128]{1,0:T(8,128)(2,1)S(1)}, bf16[512,128]{1,0:T(8,128)(2,1)S(1)}, u32[]{:S(2)}, u32[]{:S(2)}) collective-permute-start(bf16[512,128]{1,0:T(8,128)(2,1)S(1)} %get-tuple-element.107), channel_id=1, source_target_pairs={{0,24},{4,28},{8,16},{12,20},{16,8},{20,12},{24,0},{28,4},{1,25},{... | collective-permute-start | bytes 393224 | tf_op jit(solution)/shard_map/ppermute | solution.py:445
  98.1 2.5 %collective-permute-start.27 = (bf16[512,128]{1,0:T(8,128)(2,1)S(1)}, bf16[512,128]{1,0:T(8,128)(2,1)S(1)}, u32[]{:S(2)}, u32[]{:S(2)}) collective-permute-start(bf16[512,128]{1,0:T(8,128)(2,1)S(1)} %get-tuple-element.108), channel_id=1, source_target_pairs={{0,28},{4,24},{8,20},{12,16},{16,12},{20,8},{24,4},{28,0},{1,29},{... | collective-permute-start | bytes 393224 | tf_op jit(solution)/shard_map/ppermute | solution.py:445
  100.6 6.8 %shard_map.111 = (bf16[2048,512]{1,0:T(8,128)(2,1)}, f32[1024,512]{1,0:T(8,128)S(1)}, f32[1024,512]{1,0:T(8,128)S(1)}) custom-call(s32[65]{0:T(128)S(1)} %copy-done.5, s32[8]{0:T(128)S(1)} %copy-done.4, f32[4]{0:T(128)S(1)} %copy-done.3, f32[8,256]{1,0:T(8,128)S(1)} %get-tuple-element.64.refs_8_.seg_ref, bf16[2048,512]{1,0:T(8,128)(2,1)S(1)} %get-tuple-element.65.q_ref, ...), custom_call_target="tpu_custom_call" | custom-call | flops 1610612736 | tf_op jit(solution)/shard_map/pallas_call | solution.py:605
  107.4 6.2 %collective-permute-start.24 = (bf16[512,128]{1,0:T(8,128)(2,1)S(1)}, bf16[512,128]{1,0:T(8,128)(2,1)S(1)}, u32[]{:S(2)}, u32[]{:S(2)}) collective-permute-start(bf16[512,128]{1,0:T(8,128)(2,1)S(1)} %get-tuple-element.105), channel_id=1, source_target_pairs={{0,16},{4,20},{8,24},{12,28},{16,0},{20,4},{24,8},{28,12},{1,17},{... | collective-permute-start | bytes 393224 | tf_op jit(solution)/shard_map/ppermute | solution.py:445
  113.7 3.3 %collective-permute-start.28 = (bf16[512,128]{1,0:T(8,128)(2,1)S(1)}, bf16[512,128]{1,0:T(8,128)(2,1)S(1)}, u32[]{:S(2)}, u32[]{:S(2)}) collective-permute-start(bf16[512,128]{1,0:T(8,128)(2,1)S(1)} %get-tuple-element.109), channel_id=1, source_target_pairs={{0,8},{4,12},{8,0},{12,4},{16,24},{20,28},{24,16},{28,20},{1,9},{5... | collective-permute-start | bytes 393224 | tf_op jit(solution)/shard_map/ppermute | solution.py:445
  117.0 1.5 %collective-permute-start.30 = (bf16[512,128]{1,0:T(8,128)(2,1)S(1)}, bf16[512,128]{1,0:T(8,128)(2,1)S(1)}, u32[]{:S(2)}, u32[]{:S(2)}) collective-permute-start(bf16[512,128]{1,0:T(8,128)(2,1)S(1)} %get-tuple-element.112), channel_id=1, source_target_pairs={{0,4},{4,0},{8,12},{12,8},{16,20},{20,16},{24,28},{28,24},{1,5},{5... | collective-permute-start | bytes 393224 | tf_op jit(solution)/shard_map/ppermute | solution.py:445
  118.5 6.8 %shard_map.112 = (bf16[2048,512]{1,0:T(8,128)(2,1)}, f32[1024,512]{1,0:T(8,128)S(1)}, f32[1024,512]{1,0:T(8,128)S(1)}) custom-call(s32[65]{0:T(128)S(1)} %copy-done.5, s32[8]{0:T(128)S(1)} %copy-done.4, f32[4]{0:T(128)S(1)} %copy-done.3, f32[8,256]{1,0:T(8,128)S(1)} %get-tuple-element.64.refs_8_.seg_ref, ...), custom_call_target="tpu_custom_call", output_to_operand_aliasing={{0}: (16, {})} | custom-call | flops 1610612736 | tf_op jit(solution)/shard_map/pallas_call | solution.py:605
  125.4 3.8 %shard_map.114 = (bf16[2048,512]{1,0:T(8,128)(2,1)}, bf16[2048,512]{1,0:T(8,128)(2,1)}) custom-call(s32[65]{0:T(128)S(1)} %copy-done.7, s32[8]{0:T(128)S(1)} %copy-done.4, f32[4]{0:T(128)S(1)} %copy-done.3, bf16[2048,512]{1,0:T(8,128)(2,1)S(1)} %get-tuple-element.62.k_ref, bf16[2048,512]{1,0:T(8,128)(2,1)S(1)} %get-tuple-element.63.v_ref, ...), custom_call_target="tpu_custom_call" | custom-call | flops 268435456 | tf_op jit(solution)/shard_map/pallas_call | solution.py:622
  129.1 2.1 %shard_map.115 = (bf16[2048,512]{1,0:T(8,128)(2,1)}, bf16[2048,512]{1,0:T(8,128)(2,1)}) custom-call(s32[65]{0:T(128)S(1)} %copy-done.7, s32[8]{0:T(128)S(1)} %copy-done.4, f32[4]{0:T(128)S(1)} %copy-done.3, bf16[2048,512]{1,0:T(8,128)(2,1)S(1)} %get-tuple-element.62.k_ref, ...), custom_call_target="tpu_custom_call", output_to_operand_aliasing={{0}: (11, {}), {1}: (12, {})} | custom-call | flops 268435456 | tf_op jit(solution)/shard_map/pallas_call | solution.py:622
  (45 shorter events, 1.4 us)
Async XLA Ops:
  3.8 14.4 %collective-permute-start.5 = (bf16[528,128]{1,0:T(8,128)(2,1)}, bf16[528,128]{1,0:T(8,128)(2,1)S(1)}, u32[]{:S(2)}, u32[]{:S(2)}) collective-permute-start(bf16[528,128]{1,0:T(8,128)(2,1)} %get-tuple-element.74), channel_id=1, source_target_pairs={{0,24},{4,28},{8,16},{12,20},{16,8},{20,12},{24,0},{28,4},{1,25},{... | collective-permute-start | bytes 405512 | tf_op jit(solution)/shard_map/ppermute | solution.py:445
  9.0 11.5 %collective-permute-start.6 = (bf16[528,128]{1,0:T(8,128)(2,1)}, bf16[528,128]{1,0:T(8,128)(2,1)S(1)}, u32[]{:S(2)}, u32[]{:S(2)}) collective-permute-start(bf16[528,128]{1,0:T(8,128)(2,1)} %get-tuple-element.75), channel_id=1, source_target_pairs={{0,28},{4,24},{8,20},{12,16},{16,12},{20,8},{24,4},{28,0},{1,29},{... | collective-permute-start | bytes 405512 | tf_op jit(solution)/shard_map/ppermute | solution.py:445
  10.2 13.2 %copy-start.3 = (f32[4]{0:T(128)S(1)}, f32[4]{0:T(128)}, u32[]{:S(2)}) copy-start(f32[4]{0:T(128)} %rate_ref.21) | copy-start | bytes 52
  10.2 13.2 %copy-start.4 = (s32[8]{0:T(128)S(1)}, s32[8]{0:T(128)}, u32[]{:S(2)}) copy-start(s32[8]{0:T(128)} %home_ref.17) | copy-start | bytes 100
  10.2 13.2 %copy-start.8 = (s32[32]{0:T(128)S(1)}, s32[32]{0:T(128)}, u32[]{:S(2)}) copy-start(s32[32]{0:T(128)} %len_ref.1) | copy-start | bytes 388
  14.7 16.1 %collective-permute-start = (bf16[528,128]{1,0:T(8,128)(2,1)}, bf16[528,128]{1,0:T(8,128)(2,1)S(1)}, u32[]{:S(2)}, u32[]{:S(2)}) collective-permute-start(bf16[528,128]{1,0:T(8,128)(2,1)} %get-tuple-element.69), channel_id=1, source_target_pairs={{0,4},{4,0},{8,12},{12,8},{16,20},{20,16},{24,28},{28,24},{1,5},{5... | collective-permute-start | bytes 405512 | tf_op jit(solution)/shard_map/ppermute | solution.py:445
  15.1 15.7 %collective-permute-start.1 = (bf16[528,128]{1,0:T(8,128)(2,1)}, bf16[528,128]{1,0:T(8,128)(2,1)S(1)}, u32[]{:S(2)}, u32[]{:S(2)}) collective-permute-start(bf16[528,128]{1,0:T(8,128)(2,1)} %get-tuple-element.70), channel_id=1, source_target_pairs={{0,8},{4,12},{8,0},{12,4},{16,24},{20,28},{24,16},{28,20},{1,9},{5... | collective-permute-start | bytes 405512 | tf_op jit(solution)/shard_map/ppermute | solution.py:445
  15.1 15.7 %collective-permute-start.2 = (bf16[528,128]{1,0:T(8,128)(2,1)}, bf16[528,128]{1,0:T(8,128)(2,1)S(1)}, u32[]{:S(2)}, u32[]{:S(2)}) collective-permute-start(bf16[528,128]{1,0:T(8,128)(2,1)} %get-tuple-element.71), channel_id=1, source_target_pairs={{0,12},{4,8},{8,4},{12,0},{16,28},{20,24},{24,20},{28,16},{1,13},{... | collective-permute-start | bytes 405512 | tf_op jit(solution)/shard_map/ppermute | solution.py:445
  18.3 13.1 %collective-permute-start.3 = (bf16[528,128]{1,0:T(8,128)(2,1)}, bf16[528,128]{1,0:T(8,128)(2,1)S(1)}, u32[]{:S(2)}, u32[]{:S(2)}) collective-permute-start(bf16[528,128]{1,0:T(8,128)(2,1)} %get-tuple-element.72), channel_id=1, source_target_pairs={{0,16},{4,20},{8,24},{12,28},{16,0},{20,4},{24,8},{28,12},{1,17},{... | collective-permute-start | bytes 405512 | tf_op jit(solution)/shard_map/ppermute | solution.py:445
  20.5 12.9 %collective-permute-start.4 = (bf16[528,128]{1,0:T(8,128)(2,1)}, bf16[528,128]{1,0:T(8,128)(2,1)S(1)}, u32[]{:S(2)}, u32[]{:S(2)}) collective-permute-start(bf16[528,128]{1,0:T(8,128)(2,1)} %get-tuple-element.73), channel_id=1, source_target_pairs={{0,20},{4,16},{8,28},{12,24},{16,4},{20,0},{24,12},{28,8},{1,21},{... | collective-permute-start | bytes 405512 | tf_op jit(solution)/shard_map/ppermute | solution.py:445
  23.3 1.6 %copy-start = (bf16[2048,512]{1,0:T(8,128)(2,1)S(1)}, bf16[2048,512]{1,0:T(8,128)(2,1)}, u32[]{:S(2)}) copy-start(bf16[2048,512]{1,0:T(8,128)(2,1)} %q_hbm.1) | copy-start | bytes 6291460
  24.9 1.6 %copy-start.1 = (bf16[2048,512]{1,0:T(8,128)(2,1)S(1)}, bf16[2048,512]{1,0:T(8,128)(2,1)}, u32[]{:S(2)}) copy-start(bf16[2048,512]{1,0:T(8,128)(2,1)} %u_hbm.1) | copy-start | bytes 6291460
  26.5 6.8 %copy-start.2 = (bf16[528,128]{1,0:T(8,128)(2,1)S(1)}, bf16[528,128]{1,0:T(8,128)(2,1)}, u32[]{:S(2)}) copy-start(bf16[528,128]{1,0:T(8,128)(2,1)} %get-tuple-element.68.refs_0_) | copy-start | bytes 405508
  26.5 6.8 %copy-start.5 = (s32[65]{0:T(128)S(1)}, s32[65]{0:T(128)}, u32[]{:S(2)}) copy-start(s32[65]{0:T(128)} %get-tuple-element.60.first_ref) | copy-start | bytes 784
  26.5 29.2 %copy-start.6 = (f32[512]{0:T(512)S(1)}, f32[512]{0:T(512)}, u32[]{:S(2)}) copy-start(f32[512]{0:T(512)} %param.12) | copy-start | bytes 6148
  35.8 8.0 %collective-permute-start.9 = (bf16[512,128]{1,0:T(8,128)(2,1)S(1)}, bf16[512,128]{1,0:T(8,128)(2,1)S(1)}, u32[]{:S(2)}, u32[]{:S(2)}) collective-permute-start(bf16[512,128]{1,0:T(8,128)(2,1)S(1)} %get-tuple-element.78), channel_id=1, source_target_pairs={{0,24},{4,28},{8,16},{12,20},{16,8},{20,12},{24,0},{28,4},{1,25},{... | collective-permute-start | bytes 393224 | tf_op jit(solution)/shard_map/ppermute | solution.py:445
  38.3 9.1 %collective-permute-start.10 = (bf16[512,128]{1,0:T(8,128)(2,1)S(1)}, bf16[512,128]{1,0:T(8,128)(2,1)S(1)}, u32[]{:S(2)}, u32[]{:S(2)}) collective-permute-start(bf16[512,128]{1,0:T(8,128)(2,1)S(1)} %get-tuple-element.79), channel_id=1, source_target_pairs={{0,28},{4,24},{8,20},{12,16},{16,12},{20,8},{24,4},{28,0},{1,29},{... | collective-permute-start | bytes 393224 | tf_op jit(solution)/shard_map/ppermute | solution.py:445
  40.4 11.2 %collective-permute-start.11 = (bf16[512,128]{1,0:T(8,128)(2,1)S(1)}, bf16[512,128]{1,0:T(8,128)(2,1)S(1)}, u32[]{:S(2)}, u32[]{:S(2)}) collective-permute-start(bf16[512,128]{1,0:T(8,128)(2,1)S(1)} %get-tuple-element.80), channel_id=1, source_target_pairs={{0,8},{4,12},{8,0},{12,4},{16,24},{20,28},{24,16},{28,20},{1,9},{5... | collective-permute-start | bytes 393224 | tf_op jit(solution)/shard_map/ppermute | solution.py:445
  40.4 15.3 %collective-permute-start.12 = (bf16[512,128]{1,0:T(8,128)(2,1)S(1)}, bf16[512,128]{1,0:T(8,128)(2,1)S(1)}, u32[]{:S(2)}, u32[]{:S(2)}) collective-permute-start(bf16[512,128]{1,0:T(8,128)(2,1)S(1)} %get-tuple-element.81), channel_id=1, source_target_pairs={{0,12},{4,8},{8,4},{12,0},{16,28},{20,24},{24,20},{28,16},{1,13},{... | collective-permute-start | bytes 393224 | tf_op jit(solution)/shard_map/ppermute | solution.py:445
  42.6 13.1 %collective-permute-start.13 = (bf16[512,128]{1,0:T(8,128)(2,1)S(1)}, bf16[512,128]{1,0:T(8,128)(2,1)S(1)}, u32[]{:S(2)}, u32[]{:S(2)}) collective-permute-start(bf16[512,128]{1,0:T(8,128)(2,1)S(1)} %get-tuple-element.83), channel_id=1, source_target_pairs={{0,4},{4,0},{8,12},{12,8},{16,20},{20,16},{24,28},{28,24},{1,5},{5... | collective-permute-start | bytes 393224 | tf_op jit(solution)/shard_map/ppermute | solution.py:445
  43.9 14.3 %collective-permute-start.7 = (bf16[512,128]{1,0:T(8,128)(2,1)S(1)}, bf16[512,128]{1,0:T(8,128)(2,1)S(1)}, u32[]{:S(2)}, u32[]{:S(2)}) collective-permute-start(bf16[512,128]{1,0:T(8,128)(2,1)S(1)} %get-tuple-element.76), channel_id=1, source_target_pairs={{0,16},{4,20},{8,24},{12,28},{16,0},{20,4},{24,8},{28,12},{1,17},{... | collective-permute-start | bytes 393224 | tf_op jit(solution)/shard_map/ppermute | solution.py:445
  47.4 11.5 %collective-permute-start.8 = (bf16[512,128]{1,0:T(8,128)(2,1)S(1)}, bf16[512,128]{1,0:T(8,128)(2,1)S(1)}, u32[]{:S(2)}, u32[]{:S(2)}) collective-permute-start(bf16[512,128]{1,0:T(8,128)(2,1)S(1)} %get-tuple-element.77), channel_id=1, source_target_pairs={{0,20},{4,16},{8,28},{12,24},{16,4},{20,0},{24,12},{28,8},{1,21},{... | collective-permute-start | bytes 393224 | tf_op jit(solution)/shard_map/ppermute | solution.py:445
  60.3 1.9 %collective-permute-start.16 = (f32[2,8,256]{2,1,0:T(8,128)S(1)}, f32[2,8,256]{2,1,0:T(8,128)S(1)}, u32[]{:S(2)}, u32[]{:S(2)}) collective-permute-start(f32[2,8,256]{2,1,0:T(8,128)S(1)} %get-tuple-element.87.refs_3_), channel_id=1, source_target_pairs={{0,1},{1,0},{2,3},{3,2},{4,5},{5,4},{6,7},{7,6},{8,9},{9,8},{10,11... | collective-permute-start | bytes 49160 | tf_op jit(solution)/shard_map/ppermute | solution.py:445
  60.4 3.8 %collective-permute-start.15 = (f32[2,8,256]{2,1,0:T(8,128)S(1)}, f32[2,8,256]{2,1,0:T(8,128)S(1)}, u32[]{:S(2)}, u32[]{:S(2)}) collective-permute-start(f32[2,8,256]{2,1,0:T(8,128)S(1)} %get-tuple-element.87.refs_3_), channel_id=1, source_target_pairs={{0,2},{1,3},{2,0},{3,1},{4,6},{5,7},{6,4},{7,5},{8,10},{9,11},{10,... | collective-permute-start | bytes 49160 | tf_op jit(solution)/shard_map/ppermute | solution.py:445
  61.9 3.2 %collective-permute-start.14 = (f32[2,8,256]{2,1,0:T(8,128)S(1)}, f32[2,8,256]{2,1,0:T(8,128)S(1)}, u32[]{:S(2)}, u32[]{:S(2)}) collective-permute-start(f32[2,8,256]{2,1,0:T(8,128)S(1)} %get-tuple-element.87.refs_3_), channel_id=1, source_target_pairs={{0,3},{1,2},{2,1},{3,0},{4,7},{5,6},{6,5},{7,4},{8,11},{9,10},{10,... | collective-permute-start | bytes 49160 | tf_op jit(solution)/shard_map/ppermute | solution.py:445
  69.4 7.2 %collective-permute-start.17 = (bf16[512,128]{1,0:T(8,128)(2,1)S(1)}, bf16[512,128]{1,0:T(8,128)(2,1)S(1)}, u32[]{:S(2)}, u32[]{:S(2)}) collective-permute-start(bf16[512,128]{1,0:T(8,128)(2,1)S(1)} %get-tuple-element.98), channel_id=1, source_target_pairs={{0,4},{4,0},{8,12},{12,8},{16,20},{20,16},{24,28},{28,24},{1,5},{5... | collective-permute-start | bytes 393224 | tf_op jit(solution)/shard_map/ppermute | solution.py:445
  70.8 9.2 %collective-permute-start.18 = (bf16[512,128]{1,0:T(8,128)(2,1)S(1)}, bf16[512,128]{1,0:T(8,128)(2,1)S(1)}, u32[]{:S(2)}, u32[]{:S(2)}) collective-permute-start(bf16[512,128]{1,0:T(8,128)(2,1)S(1)} %get-tuple-element.99), channel_id=1, source_target_pairs={{0,8},{4,12},{8,0},{12,4},{16,24},{20,28},{24,16},{28,20},{1,9},{5... | collective-permute-start | bytes 393224 | tf_op jit(solution)/shard_map/ppermute | solution.py:445
  70.8 11.6 %collective-permute-start.19 = (bf16[512,128]{1,0:T(8,128)(2,1)S(1)}, bf16[512,128]{1,0:T(8,128)(2,1)S(1)}, u32[]{:S(2)}, u32[]{:S(2)}) collective-permute-start(bf16[512,128]{1,0:T(8,128)(2,1)S(1)} %get-tuple-element.100), channel_id=1, source_target_pairs={{0,12},{4,8},{8,4},{12,0},{16,28},{20,24},{24,20},{28,16},{1,13},{... | collective-permute-start | bytes 393224 | tf_op jit(solution)/shard_map/ppermute | solution.py:445
  73.0 18.5 %collective-permute-start.20 = (bf16[512,128]{1,0:T(8,128)(2,1)S(1)}, bf16[512,128]{1,0:T(8,128)(2,1)S(1)}, u32[]{:S(2)}, u32[]{:S(2)}) collective-permute-start(bf16[512,128]{1,0:T(8,128)(2,1)S(1)} %get-tuple-element.101), channel_id=1, source_target_pairs={{0,16},{4,20},{8,24},{12,28},{16,0},{20,4},{24,8},{28,12},{1,17},{... | collective-permute-start | bytes 393224 | tf_op jit(solution)/shard_map/ppermute | solution.py:445
  73.4 21.6 %collective-permute-start.21 = (bf16[512,128]{1,0:T(8,128)(2,1)S(1)}, bf16[512,128]{1,0:T(8,128)(2,1)S(1)}, u32[]{:S(2)}, u32[]{:S(2)}) collective-permute-start(bf16[512,128]{1,0:T(8,128)(2,1)S(1)} %get-tuple-element.102), channel_id=1, source_target_pairs={{0,20},{4,16},{8,28},{12,24},{16,4},{20,0},{24,12},{28,8},{1,21},{... | collective-permute-start | bytes 393224 | tf_op jit(solution)/shard_map/ppermute | solution.py:445
  76.6 18.4 %collective-permute-start.22 = (bf16[512,128]{1,0:T(8,128)(2,1)S(1)}, bf16[512,128]{1,0:T(8,128)(2,1)S(1)}, u32[]{:S(2)}, u32[]{:S(2)}) collective-permute-start(bf16[512,128]{1,0:T(8,128)(2,1)S(1)} %get-tuple-element.103), channel_id=1, source_target_pairs={{0,24},{4,28},{8,16},{12,20},{16,8},{20,12},{24,0},{28,4},{1,25},{... | collective-permute-start | bytes 393224 | tf_op jit(solution)/shard_map/ppermute | solution.py:445
  80.0 15.0 %collective-permute-start.23 = (bf16[512,128]{1,0:T(8,128)(2,1)S(1)}, bf16[512,128]{1,0:T(8,128)(2,1)S(1)}, u32[]{:S(2)}, u32[]{:S(2)}) collective-permute-start(bf16[512,128]{1,0:T(8,128)(2,1)S(1)} %get-tuple-element.104), channel_id=1, source_target_pairs={{0,28},{4,24},{8,20},{12,16},{16,12},{20,8},{24,4},{28,0},{1,29},{... | collective-permute-start | bytes 393224 | tf_op jit(solution)/shard_map/ppermute | solution.py:445
  96.5 20.5 %collective-permute-start.26 = (bf16[512,128]{1,0:T(8,128)(2,1)S(1)}, bf16[512,128]{1,0:T(8,128)(2,1)S(1)}, u32[]{:S(2)}, u32[]{:S(2)}) collective-permute-start(bf16[512,128]{1,0:T(8,128)(2,1)S(1)} %get-tuple-element.107), channel_id=1, source_target_pairs={{0,24},{4,28},{8,16},{12,20},{16,8},{20,12},{24,0},{28,4},{1,25},{... | collective-permute-start | bytes 393224 | tf_op jit(solution)/shard_map/ppermute | solution.py:445
  98.1 18.9 %collective-permute-start.27 = (bf16[512,128]{1,0:T(8,128)(2,1)S(1)}, bf16[512,128]{1,0:T(8,128)(2,1)S(1)}, u32[]{:S(2)}, u32[]{:S(2)}) collective-permute-start(bf16[512,128]{1,0:T(8,128)(2,1)S(1)} %get-tuple-element.108), channel_id=1, source_target_pairs={{0,28},{4,24},{8,20},{12,16},{16,12},{20,8},{24,4},{28,0},{1,29},{... | collective-permute-start | bytes 393224 | tf_op jit(solution)/shard_map/ppermute | solution.py:445
  107.4 21.7 %collective-permute-start.24 = (bf16[512,128]{1,0:T(8,128)(2,1)S(1)}, bf16[512,128]{1,0:T(8,128)(2,1)S(1)}, u32[]{:S(2)}, u32[]{:S(2)}) collective-permute-start(bf16[512,128]{1,0:T(8,128)(2,1)S(1)} %get-tuple-element.105), channel_id=1, source_target_pairs={{0,16},{4,20},{8,24},{12,28},{16,0},{20,4},{24,8},{28,12},{1,17},{... | collective-permute-start | bytes 393224 | tf_op jit(solution)/shard_map/ppermute | solution.py:445
  113.6 15.6 %collective-permute-start.25 = (bf16[512,128]{1,0:T(8,128)(2,1)S(1)}, bf16[512,128]{1,0:T(8,128)(2,1)S(1)}, u32[]{:S(2)}, u32[]{:S(2)}) collective-permute-start(bf16[512,128]{1,0:T(8,128)(2,1)S(1)} %get-tuple-element.106), channel_id=1, source_target_pairs={{0,20},{4,16},{8,28},{12,24},{16,4},{20,0},{24,12},{28,8},{1,21},{... | collective-permute-start | bytes 393224 | tf_op jit(solution)/shard_map/ppermute | solution.py:445
  113.7 11.7 %collective-permute-start.28 = (bf16[512,128]{1,0:T(8,128)(2,1)S(1)}, bf16[512,128]{1,0:T(8,128)(2,1)S(1)}, u32[]{:S(2)}, u32[]{:S(2)}) collective-permute-start(bf16[512,128]{1,0:T(8,128)(2,1)S(1)} %get-tuple-element.109), channel_id=1, source_target_pairs={{0,8},{4,12},{8,0},{12,4},{16,24},{20,28},{24,16},{28,20},{1,9},{5... | collective-permute-start | bytes 393224 | tf_op jit(solution)/shard_map/ppermute | solution.py:445
  117.0 8.3 %collective-permute-start.29 = (bf16[512,128]{1,0:T(8,128)(2,1)S(1)}, bf16[512,128]{1,0:T(8,128)(2,1)S(1)}, u32[]{:S(2)}, u32[]{:S(2)}) collective-permute-start(bf16[512,128]{1,0:T(8,128)(2,1)S(1)} %get-tuple-element.110), channel_id=1, source_target_pairs={{0,12},{4,8},{8,4},{12,0},{16,28},{20,24},{24,20},{28,16},{1,13},{... | collective-permute-start | bytes 393224 | tf_op jit(solution)/shard_map/ppermute | solution.py:445
  117.0 8.3 %collective-permute-start.30 = (bf16[512,128]{1,0:T(8,128)(2,1)S(1)}, bf16[512,128]{1,0:T(8,128)(2,1)S(1)}, u32[]{:S(2)}, u32[]{:S(2)}) collective-permute-start(bf16[512,128]{1,0:T(8,128)(2,1)S(1)} %get-tuple-element.112), channel_id=1, source_target_pairs={{0,4},{4,0},{8,12},{12,8},{16,20},{20,16},{24,28},{28,24},{1,5},{5... | collective-permute-start | bytes 393224 | tf_op jit(solution)/shard_map/ppermute | solution.py:445
  118.5 6.9 %copy-start.7 = (s32[65]{0:T(128)S(1)}, s32[65]{0:T(128)}, u32[]{:S(2)}) copy-start(s32[65]{0:T(128)} %get-tuple-element.61.refs_0_.last_ref) | copy-start | bytes 784
where the time goes:
time: 132 us; the launch traced here: 131 us
  starting transfers between devices  54.3 us (41%)
  Pallas kernels  43.7 us (33%)
  waiting for transfers between devices  29.2 us (22%)
  local copies, waits for them, and re-layouts  3.2 us (2%)
    ppermute x31, starting transfers between devices, swap(): lax.ppermute(array, axis, [(i, i ^ mask) for i in range(lax.axis_size(axi...  54.3 us
    ppermute x31, waiting for transfers between devices, swap(): lax.ppermute(array, axis, [(i, i ^ mask) for i in range(lax.axis_size(axi...  29.2 us
    pallas_call x2, Pallas kernels, inner_grads(): call(inner_grads_kernel, LIMIT, 3 * work, [smem, smem, smem, vmem, vmem,...  13.7 us
    pallas_call x2, Pallas kernels, outer_grads(): call(outer_grads_kernel, LIMIT, work // 2, [smem, smem, smem] + [vmem] *...  5.83 us
    pallas_call x1, Pallas kernels, shards(): call(summary_kernel, ALONE, work // 2, [smem, smem, smem, hbm, hbm], [vme...  4.53 us
    pallas_call x1, Pallas kernels, shards(): call(local_kernel, LIMIT, 2 * work, [smem, smem, smem, hbm, hbm, vmem, vm...  4.3 us
    pallas_call x2, Pallas kernels, cotangents(): call(cotangent_kernel, LIMIT, work // 4, [smem, smem, smem] + [vmem] * (4...  4.29 us
    pallas_call x2, Pallas kernels, scan(): call(scan_kernel, LIMIT, work // 8, [smem, smem, smem] + taken + [hbm] *...  3.97 us
  transfers between devices with their start and end apart: 31, of which 11 were waited for; matrix products, arithmetic and copies ran while one was open for 0% of the time, Pallas kernels for 22%

commit v1 on v0

--- a/solution.py
+++ b/solution.py
@@ -230,15 +230,16 @@
         arrived, states = refs
     else:
         order_ref, arrived, states, homes, home_ref, home_sem = refs
-    slots = states.shape[1] // rows
     spans = order_ref.shape[0]
+    slots = spans // count
+    size = slots * rows
     if not reverse:
         for k, ref in enumerate(sources):
             homes[k : k + 1, :] = ref[slots * rows :, :].astype(F32)[0:1].astype(jnp.int32)
         gather = pltpu.make_async_copy(homes, home_ref, home_sem)
         gather.start()
     for k, ref in enumerate(sources):
-        arrived[k] = ref[: slots * rows]
+        arrived[k * size : (k + 1) * size] = ref[:size]
     head = (own_index() * rows) // HEAD_SIZE
     factor = jnp.exp(jnp.full((8, LANES), -rate_ref[head] * span, F32))[0:1]
     if not reverse:
@@ -249,20 +250,19 @@
                 order_ref[home_ref[k, i]] = k * slots + i
             return carry
 
-        lax.fori_loop(0, count, note, 0)
+        lax.fori_loop(0, count, note, 0, unroll=2)
 
     def body(i, state):
         c = spans - 1 - i if reverse else i
         place = order_ref[c]
-        block, slot = place // slots, place % slots
-        at = rows_at(slot, rows)
-        states[block, at, :] = state.astype(BF16)
+        at = rows_at(place, rows)
+        states[at, :] = state.astype(BF16)
         carried = jnp.where(first_ref[c] >= span, factor * state, 0.0)
-        return carried + arrived[block, at, :].astype(F32)
-
-    lax.fori_loop(0, spans, body, jnp.zeros((rows, LANES), F32), unroll=4)
+        return carried + arrived[at, :].astype(F32)
+
+    lax.fori_loop(0, spans, body, jnp.zeros((rows, LANES), F32), unroll=8)
     for k, ref in enumerate(targets):
-        ref[...] = states[k]
+        ref[...] = states[k * size : (k + 1) * size]
 
 
 def local_kernel(
@@ -544,7 +544,7 @@
     )(document_lengths, group_home, decay_rate, query, upstream, key_v, value_v)
 
     def scan(arrived, order, reverse, *after_it):
-        held = [states, states]
+        held = [pltpu.VMEM((devices * slots * rows, LANES), BF16)] * 2
         if reverse:
             extra_specs, extra = [], []
         else:

time: 132 us -> 133 us (level)
  starting transfers between devices: 54.3 us -> 56 us
    ppermute x31, starting transfers between devices: 54.3 us -> 56 us  [swap(): lax.ppermute(array, axis, [(i, i ^ mask) for i in range(lax.axis_size(axi...]
where the time goes in v1:
time: 133 us
  starting transfers between devices  56 us (42%)
  Pallas kernels  43.2 us (32%)
  waiting for transfers between devices  29.2 us (22%)
  local copies, waits for them, and re-layouts  3.2 us (2%)
    ppermute x31, starting transfers between devices, swap(): lax.ppermute(array, axis, [(i, i ^ mask) for i in range(lax.axis_size(axi...  56 us
    ppermute x31, waiting for transfers between devices, swap(): lax.ppermute(array, axis, [(i, i ^ mask) for i in range(lax.axis_size(axi...  29.2 us
    pallas_call x2, Pallas kernels, inner_grads(): call(inner_grads_kernel, LIMIT, 3 * work, [smem, smem, smem, vmem, vmem,...  13.7 us
    pallas_call x2, Pallas kernels, outer_grads(): call(outer_grads_kernel, LIMIT, work // 2, [smem, smem, smem] + [vmem] *...  5.83 us
    pallas_call x1, Pallas kernels, shards(): call(summary_kernel, ALONE, work // 2, [smem, smem, smem, hbm, hbm], [vme...  4.53 us
    pallas_call x1, Pallas kernels, shards(): call(local_kernel, LIMIT, 2 * work, [smem, smem, smem, hbm, hbm, vmem, vm...  4.3 us
    pallas_call x2, Pallas kernels, cotangents(): call(cotangent_kernel, LIMIT, work // 4, [smem, smem, smem] + [vmem] * (4...  4.3 us
    pallas_call x2, Pallas kernels, outputs(): call(output_kernel, LIMIT, work // 4, [smem, smem, smem] + [vmem] * (4 +...  3.87 us
  transfers between devices with their start and end apart: 31, of which 11 were waited for; matrix products, arithmetic and copies ran while one was open for 0% of the time, Pallas kernels for 22%

profile of v1, /device:TPU:0, one launch (start us, length us, event | category | flops | bytes accessed | tf_op | source)
XLA Modules:
  0.0 132.5 jit_solution(8151361717335716486)
XLA Ops:
  0.6 3.2 %shard_map.103 = (bf16[528,128]{1,0:T(8,128)(2,1)}, bf16[528,128]{1,0:T(8,128)(2,1)}, s32[65]{0:T(128)}, s32[65]{0:T(128)}) custom-call(s32[32]{0:T(128)} %len_ref.1, s32[8]{0:T(128)} %home_ref.17, f32[4]{0:T(128)} %rate_ref.21, bf16[2048,512]{1,0:T(8,128)(2,1)} %refs_3_.3, bf16[2048,512]{1,0:T(8,128)(2,1)} %refs_4_.3), custom_call_target="tpu_custom_call" | custom-call | flops 67108864 | tf_op jit(solution)/shard_map/pallas_call | solution.py:516
  3.8 5.1 %collective-permute-start.5 = (bf16[528,128]{1,0:T(8,128)(2,1)}, bf16[528,128]{1,0:T(8,128)(2,1)S(1)}, u32[]{:S(2)}, u32[]{:S(2)}) collective-permute-start(bf16[528,128]{1,0:T(8,128)(2,1)} %get-tuple-element.74), channel_id=1, source_target_pairs={{0,24},{4,28},{8,16},{12,20},{16,8},{20,12},{24,0},{28,4},{1,25},{... | collective-permute-start | bytes 405512 | tf_op jit(solution)/shard_map/ppermute | solution.py:445
  9.0 1.2 collective-permute-start.6
  10.2 4.5 %shard_map.104 = (bf16[528,128]{1,0:T(8,128)(2,1)}, bf16[528,128]{1,0:T(8,128)(2,1)}, bf16[528,128]{1,0:T(8,128)(2,1)}, bf16[528,128]{1,0:T(8,128)(2,1)}, bf16[5...) custom-call(s32[65]{0:T(128)} %get-tuple-element.61.refs_0_.last_ref, ...), custom_call_target="tpu_custom_call" | custom-call | flops 268435456 | tf_op jit(solution)/shard_map/pallas_call | solution.py:526
  15.1 3.1 %collective-permute-start.2 = (bf16[528,128]{1,0:T(8,128)(2,1)}, bf16[528,128]{1,0:T(8,128)(2,1)S(1)}, u32[]{:S(2)}, u32[]{:S(2)}) collective-permute-start(bf16[528,128]{1,0:T(8,128)(2,1)} %get-tuple-element.71), channel_id=1, source_target_pairs={{0,12},{4,8},{8,4},{12,0},{16,28},{20,24},{24,20},{28,16},{1,13},{... | collective-permute-start | bytes 405512 | tf_op jit(solution)/shard_map/ppermute | solution.py:445
  18.3 2.2 %collective-permute-start.3 = (bf16[528,128]{1,0:T(8,128)(2,1)}, bf16[528,128]{1,0:T(8,128)(2,1)S(1)}, u32[]{:S(2)}, u32[]{:S(2)}) collective-permute-start(bf16[528,128]{1,0:T(8,128)(2,1)} %get-tuple-element.72), channel_id=1, source_target_pairs={{0,16},{4,20},{8,24},{12,28},{16,0},{20,4},{24,8},{28,12},{1,17},{... | collective-permute-start | bytes 405512 | tf_op jit(solution)/shard_map/ppermute | solution.py:445
  20.5 2.9 %collective-permute-start.4 = (bf16[528,128]{1,0:T(8,128)(2,1)}, bf16[528,128]{1,0:T(8,128)(2,1)S(1)}, u32[]{:S(2)}, u32[]{:S(2)}) collective-permute-start(bf16[528,128]{1,0:T(8,128)(2,1)} %get-tuple-element.73), channel_id=1, source_target_pairs={{0,20},{4,16},{8,28},{12,24},{16,4},{20,0},{24,12},{28,8},{1,21},{... | collective-permute-start | bytes 405512 | tf_op jit(solution)/shard_map/ppermute | solution.py:445
  23.3 1.6 %copy-done = bf16[2048,512]{1,0:T(8,128)(2,1)S(1)} copy-done((bf16[2048,512]{1,0:T(8,128)(2,1)S(1)}, bf16[2048,512]{1,0:T(8,128)(2,1)}, u32[]{:S(2)}) %copy-start) | copy-done | bytes 2097176
  24.9 1.6 %copy-done.1 = bf16[2048,512]{1,0:T(8,128)(2,1)S(1)} copy-done((bf16[2048,512]{1,0:T(8,128)(2,1)S(1)}, bf16[2048,512]{1,0:T(8,128)(2,1)}, u32[]{:S(2)}) %copy-start.1) | copy-done | bytes 2097176
  26.5 4.3 %shard_map.105 = (f32[2048,512]{1,0:T(8,128)S(1)}, bf16[2048,512]{1,0:T(8,128)(2,1)S(1)}, bf16[2048,512]{1,0:T(8,128)(2,1)S(1)}, f32[8,256]{1,0:T(8,128)S(1)}) custom-call(s32[32]{0:T(128)S(1)} %copy-done.8, s32[8]{0:T(128)S(1)} %copy-done.4, f32[4]{0:T(128)S(1)} %copy-done.3, bf16[2048,512]{1,0:T(8,128)(2,1)S(1)} %copy-done, ...), custom_call_target="tpu_custom_call" | custom-call | flops 1073741824 | tf_op jit(solution)/shard_map/pallas_call | solution.py:537
  30.9 0.5 collective-permute-done.3.refs_4_
  31.4 2.0 %collective-permute-done.4.refs_5_ = bf16[528,128]{1,0:T(8,128)(2,1)S(1)} collective-permute-done((bf16[528,128]{1,0:T(8,128)(2,1)}, bf16[528,128]{1,0:T(8,128)(2,1)S(1)}, u32[]{:S(2)}, u32[]{:S(2)}) %collective-permute-start.4) | collective-permute-done | bytes 135200 | tf_op jit(solution)/shard_map/ppermute | solution.py:445
  33.3 2.2 %shard_map.106 = (bf16[512,128]{1,0:T(8,128)(2,1)S(1)}, bf16[512,128]{1,0:T(8,128)(2,1)S(1)}, bf16[512,128]{1,0:T(8,128)(2,1)S(1)}, bf16[512,128]{1,0:T(8,128)(2...) custom-call(s32[65]{0:T(128)S(1)} %copy-done.5, ...), custom_call_target="tpu_custom_call" | custom-call | flops 67108864 | tf_op jit(solution)/shard_map/pallas_call | solution.py:554
  35.6 2.5 %collective-permute-start.9 = (bf16[512,128]{1,0:T(8,128)(2,1)S(1)}, bf16[512,128]{1,0:T(8,128)(2,1)S(1)}, u32[]{:S(2)}, u32[]{:S(2)}) collective-permute-start(bf16[512,128]{1,0:T(8,128)(2,1)S(1)} %get-tuple-element.78), channel_id=1, source_target_pairs={{0,24},{4,28},{8,16},{12,20},{16,8},{20,12},{24,0},{28,4},{1,25},{... | collective-permute-start | bytes 393224 | tf_op jit(solution)/shard_map/ppermute | solution.py:445
  38.1 2.0 %collective-permute-start.10 = (bf16[512,128]{1,0:T(8,128)(2,1)S(1)}, bf16[512,128]{1,0:T(8,128)(2,1)S(1)}, u32[]{:S(2)}, u32[]{:S(2)}) collective-permute-start(bf16[512,128]{1,0:T(8,128)(2,1)S(1)} %get-tuple-element.79), channel_id=1, source_target_pairs={{0,28},{4,24},{8,20},{12,16},{16,12},{20,8},{24,4},{28,0},{1,29},{... | collective-permute-start | bytes 393224 | tf_op jit(solution)/shard_map/ppermute | solution.py:445
  40.1 2.3 %collective-permute-start.12 = (bf16[512,128]{1,0:T(8,128)(2,1)S(1)}, bf16[512,128]{1,0:T(8,128)(2,1)S(1)}, u32[]{:S(2)}, u32[]{:S(2)}) collective-permute-start(bf16[512,128]{1,0:T(8,128)(2,1)S(1)} %get-tuple-element.81), channel_id=1, source_target_pairs={{0,12},{4,8},{8,4},{12,0},{16,28},{20,24},{24,20},{28,16},{1,13},{... | collective-permute-start | bytes 393224 | tf_op jit(solution)/shard_map/ppermute | solution.py:445
  42.4 1.2 collective-permute-start.13
  43.6 1.1 collective-permute-start.7
  44.7 2.4 %collective-permute-done.10.refs_1_.refs_7_ = bf16[512,128]{1,0:T(8,128)(2,1)S(1)} collective-permute-done((bf16[512,128]{1,0:T(8,128)(2,1)S(1)}, bf16[512,128]{1,0:T(8,128)(2,1)S(1)}, u32[]{:S(2)}, u32[]{:S(2)}) %collective-permute-start.10) | collective-permute-done | bytes 131104 | tf_op jit(solution)/shard_map/ppermute | solution.py:445
  47.1 2.2 %collective-permute-start.8 = (bf16[512,128]{1,0:T(8,128)(2,1)S(1)}, bf16[512,128]{1,0:T(8,128)(2,1)S(1)}, u32[]{:S(2)}, u32[]{:S(2)}) collective-permute-start(bf16[512,128]{1,0:T(8,128)(2,1)S(1)} %get-tuple-element.77), channel_id=1, source_target_pairs={{0,20},{4,16},{8,28},{12,24},{16,4},{20,0},{24,12},{28,8},{1,21},{... | collective-permute-start | bytes 393224 | tf_op jit(solution)/shard_map/ppermute | solution.py:445
  49.4 1.9 %collective-permute-done.11.refs_2_ = bf16[512,128]{1,0:T(8,128)(2,1)S(1)} collective-permute-done((bf16[512,128]{1,0:T(8,128)(2,1)S(1)}, bf16[512,128]{1,0:T(8,128)(2,1)S(1)}, u32[]{:S(2)}, u32[]{:S(2)}) %collective-permute-start.11) | collective-permute-done | bytes 131104 | tf_op jit(solution)/shard_map/ppermute | solution.py:445
  51.3 4.2 %collective-permute-done.12.refs_3_ = bf16[512,128]{1,0:T(8,128)(2,1)S(1)} collective-permute-done((bf16[512,128]{1,0:T(8,128)(2,1)S(1)}, bf16[512,128]{1,0:T(8,128)(2,1)S(1)}, u32[]{:S(2)}, u32[]{:S(2)}) %collective-permute-start.12) | collective-permute-done | bytes 131104 | tf_op jit(solution)/shard_map/ppermute | solution.py:445
  55.4 2.5 %shard_map.107 = (f32[2048,512]{1,0:T(8,128)S(1)}, f32[2,8,256]{2,1,0:T(8,128)S(1)}) custom-call(s32[65]{0:T(128)S(1)} %copy-done.5, s32[8]{0:T(128)S(1)} %copy-done.4, f32[4]{0:T(128)S(1)} %copy-done.3, f32[1,512]{1,0:T(1,128)S(1)} %bitcast.1, bf16[2048,512]{1,0:T(8,128)(2,1)S(1)} %get-tuple-element.65.q_ref, ...), custom_call_target="tpu_custom_call" | custom-call | flops 134217728 | tf_op jit(solution)/shard_map/pallas_call | solution.py:569
  57.9 0.7 collective-permute-done.8.refs_1_.refs_5_
  58.6 1.4 %shard_map.108 = (f32[2048,512]{1,0:T(8,128)S(1)}, f32[2,8,256]{2,1,0:T(8,128)S(1)}) custom-call(s32[65]{0:T(128)S(1)} %copy-done.5, s32[8]{0:T(128)S(1)} %copy-done.4, f32[4]{0:T(128)S(1)} %copy-done.3, f32[1,512]{1,0:T(1,128)S(1)} %bitcast.2, bf16[2048,512]{1,0:T(8,128)(2,1)S(1)} %get-tuple-element.65.q_ref, ...), custom_call_target="tpu_custom_call", output_to_operand_aliasing={{0}: (10, {})} | custom-call | flops 134217728 | tf_op jit(solution)/shard_map/pallas_call | solution.py:569
  60.1 1.6 %collective-permute-start.15 = (f32[2,8,256]{2,1,0:T(8,128)S(1)}, f32[2,8,256]{2,1,0:T(8,128)S(1)}, u32[]{:S(2)}, u32[]{:S(2)}) collective-permute-start(f32[2,8,256]{2,1,0:T(8,128)S(1)} %get-tuple-element.87.refs_3_), channel_id=1, source_target_pairs={{0,2},{1,3},{2,0},{3,1},{4,6},{5,7},{6,4},{7,5},{8,10},{9,11},{10,... | collective-permute-start | bytes 49160 | tf_op jit(solution)/shard_map/ppermute | solution.py:445
  61.9 2.0 %collective-permute-done.15.refs_1_ = f32[2,8,256]{2,1,0:T(8,128)S(1)} collective-permute-done((f32[2,8,256]{2,1,0:T(8,128)S(1)}, f32[2,8,256]{2,1,0:T(8,128)S(1)}, u32[]{:S(2)}, u32[]{:S(2)}) %collective-permute-start.15) | collective-permute-done | bytes 16416 | tf_op jit(solution)/shard_map/ppermute | solution.py:445
  63.9 0.9 collective-permute-done.14.refs_0_
  64.8 1.7 %shard_map.109 = (bf16[2048,512]{1,0:T(8,128)(2,1)S(1)}, bf16[512,128]{1,0:T(8,128)(2,1)S(1)}, bf16[512,128]{1,0:T(8,128)(2,1)S(1)}) custom-call(s32[65]{0:T(128)S(1)} %copy-done.5, s32[8]{0:T(128)S(1)} %copy-done.4, f32[4]{0:T(128)S(1)} %copy-done.3, f32[1,512]{1,0:T(1,128)S(1)} %bitcast.3, bf16[2048,512]{1,0:T(8,128)(2,1)S(1)} %get-tuple-element.65.q_ref, ...), custom_call_target="tpu_custom_call" | custom-call | flops 134217728 | tf_op jit(solution)/shard_map/pallas_call | solution.py:586
  66.5 2.6 %shard_map.110 = (bf16[2048,512]{1,0:T(8,128)(2,1)S(1)}, bf16[512,128]{1,0:T(8,128)(2,1)S(1)}, bf16[512,128]{1,0:T(8,128)(2,1)S(1)}, bf16[512,128]{1,0:T(8,128)(...) custom-call(s32[65]{0:T(128)S(1)} %copy-done.5, ...), custom_call_target="tpu_custom_call", output_to_operand_aliasing={{0}: (11, {})} | custom-call | flops 134217728 | tf_op jit(solution)/shard_map/pallas_call | solution.py:586
  69.1 1.4 %collective-permute-start.17 = (bf16[512,128]{1,0:T(8,128)(2,1)S(1)}, bf16[512,128]{1,0:T(8,128)(2,1)S(1)}, u32[]{:S(2)}, u32[]{:S(2)}) collective-permute-start(bf16[512,128]{1,0:T(8,128)(2,1)S(1)} %get-tuple-element.98), channel_id=1, source_target_pairs={{0,4},{4,0},{8,12},{12,8},{16,20},{20,16},{24,28},{28,24},{1,5},{5... | collective-permute-start | bytes 393224 | tf_op jit(solution)/shard_map/ppermute | solution.py:445
  70.5 2.2 %collective-permute-start.19 = (bf16[512,128]{1,0:T(8,128)(2,1)S(1)}, bf16[512,128]{1,0:T(8,128)(2,1)S(1)}, u32[]{:S(2)}, u32[]{:S(2)}) collective-permute-start(bf16[512,128]{1,0:T(8,128)(2,1)S(1)} %get-tuple-element.100), channel_id=1, source_target_pairs={{0,12},{4,8},{8,4},{12,0},{16,28},{20,24},{24,20},{28,16},{1,13},{... | collective-permute-start | bytes 393224 | tf_op jit(solution)/shard_map/ppermute | solution.py:445
  73.1 3.2 %collective-permute-start.21 = (bf16[512,128]{1,0:T(8,128)(2,1)S(1)}, bf16[512,128]{1,0:T(8,128)(2,1)S(1)}, u32[]{:S(2)}, u32[]{:S(2)}) collective-permute-start(bf16[512,128]{1,0:T(8,128)(2,1)S(1)} %get-tuple-element.102), channel_id=1, source_target_pairs={{0,20},{4,16},{8,28},{12,24},{16,4},{20,0},{24,12},{28,8},{1,21},{... | collective-permute-start | bytes 393224 | tf_op jit(solution)/shard_map/ppermute | solution.py:445
  76.4 1.5 %collective-permute-start.22 = (bf16[512,128]{1,0:T(8,128)(2,1)S(1)}, bf16[512,128]{1,0:T(8,128)(2,1)S(1)}, u32[]{:S(2)}, u32[]{:S(2)}) collective-permute-start(bf16[512,128]{1,0:T(8,128)(2,1)S(1)} %get-tuple-element.103), channel_id=1, source_target_pairs={{0,24},{4,28},{8,16},{12,20},{16,8},{20,12},{24,0},{28,4},{1,25},{... | collective-permute-start | bytes 393224 | tf_op jit(solution)/shard_map/ppermute | solution.py:445
  77.8 1.9 %collective-permute-done.18.refs_2_ = bf16[512,128]{1,0:T(8,128)(2,1)S(1)} collective-permute-done((bf16[512,128]{1,0:T(8,128)(2,1)S(1)}, bf16[512,128]{1,0:T(8,128)(2,1)S(1)}, u32[]{:S(2)}, u32[]{:S(2)}) %collective-permute-start.18) | collective-permute-done | bytes 131104 | tf_op jit(solution)/shard_map/ppermute | solution.py:445
  79.7 2.3 %collective-permute-start.23 = (bf16[512,128]{1,0:T(8,128)(2,1)S(1)}, bf16[512,128]{1,0:T(8,128)(2,1)S(1)}, u32[]{:S(2)}, u32[]{:S(2)}) collective-permute-start(bf16[512,128]{1,0:T(8,128)(2,1)S(1)} %get-tuple-element.104), channel_id=1, source_target_pairs={{0,28},{4,24},{8,20},{12,16},{16,12},{20,8},{24,4},{28,0},{1,29},{... | collective-permute-start | bytes 393224 | tf_op jit(solution)/shard_map/ppermute | solution.py:445
  82.1 9.1 %collective-permute-done.20.refs_4_ = bf16[512,128]{1,0:T(8,128)(2,1)S(1)} collective-permute-done((bf16[512,128]{1,0:T(8,128)(2,1)S(1)}, bf16[512,128]{1,0:T(8,128)(2,1)S(1)}, u32[]{:S(2)}, u32[]{:S(2)}) %collective-permute-start.20) | collective-permute-done | bytes 131104 | tf_op jit(solution)/shard_map/ppermute | solution.py:445
  91.2 3.5 %collective-permute-done.21.refs_5_ = bf16[512,128]{1,0:T(8,128)(2,1)S(1)} collective-permute-done((bf16[512,128]{1,0:T(8,128)(2,1)S(1)}, bf16[512,128]{1,0:T(8,128)(2,1)S(1)}, u32[]{:S(2)}, u32[]{:S(2)}) %collective-permute-start.21) | collective-permute-done | bytes 131104 | tf_op jit(solution)/shard_map/ppermute | solution.py:445
  94.7 1.2 shard_map.113
  96.0 1.5 %collective-permute-start.26 = (bf16[512,128]{1,0:T(8,128)(2,1)S(1)}, bf16[512,128]{1,0:T(8,128)(2,1)S(1)}, u32[]{:S(2)}, u32[]{:S(2)}) collective-permute-start(bf16[512,128]{1,0:T(8,128)(2,1)S(1)} %get-tuple-element.107), channel_id=1, source_target_pairs={{0,24},{4,28},{8,16},{12,20},{16,8},{20,12},{24,0},{28,4},{1,25},{... | collective-permute-start | bytes 393224 | tf_op jit(solution)/shard_map/ppermute | solution.py:445
  97.5 2.5 %collective-permute-start.27 = (bf16[512,128]{1,0:T(8,128)(2,1)S(1)}, bf16[512,128]{1,0:T(8,128)(2,1)S(1)}, u32[]{:S(2)}, u32[]{:S(2)}) collective-permute-start(bf16[512,128]{1,0:T(8,128)(2,1)S(1)} %get-tuple-element.108), channel_id=1, source_target_pairs={{0,28},{4,24},{8,20},{12,16},{16,12},{20,8},{24,4},{28,0},{1,29},{... | collective-permute-start | bytes 393224 | tf_op jit(solution)/shard_map/ppermute | solution.py:445
  100.1 6.8 %shard_map.111 = (bf16[2048,512]{1,0:T(8,128)(2,1)}, f32[1024,512]{1,0:T(8,128)S(1)}, f32[1024,512]{1,0:T(8,128)S(1)}) custom-call(s32[65]{0:T(128)S(1)} %copy-done.5, s32[8]{0:T(128)S(1)} %copy-done.4, f32[4]{0:T(128)S(1)} %copy-done.3, f32[8,256]{1,0:T(8,128)S(1)} %get-tuple-element.64.refs_8_.seg_ref, bf16[2048,512]{1,0:T(8,128)(2,1)S(1)} %get-tuple-element.65.q_ref, ...), custom_call_target="tpu_custom_call" | custom-call | flops 1610612736 | tf_op jit(solution)/shard_map/pallas_call | solution.py:605
  106.9 7.8 %collective-permute-start.24 = (bf16[512,128]{1,0:T(8,128)(2,1)S(1)}, bf16[512,128]{1,0:T(8,128)(2,1)S(1)}, u32[]{:S(2)}, u32[]{:S(2)}) collective-permute-start(bf16[512,128]{1,0:T(8,128)(2,1)S(1)} %get-tuple-element.105), channel_id=1, source_target_pairs={{0,16},{4,20},{8,24},{12,28},{16,0},{20,4},{24,8},{28,12},{1,17},{... | collective-permute-start | bytes 393224 | tf_op jit(solution)/shard_map/ppermute | solution.py:445
  114.8 3.3 %collective-permute-start.28 = (bf16[512,128]{1,0:T(8,128)(2,1)S(1)}, bf16[512,128]{1,0:T(8,128)(2,1)S(1)}, u32[]{:S(2)}, u32[]{:S(2)}) collective-permute-start(bf16[512,128]{1,0:T(8,128)(2,1)S(1)} %get-tuple-element.109), channel_id=1, source_target_pairs={{0,8},{4,12},{8,0},{12,4},{16,24},{20,28},{24,16},{28,20},{1,9},{5... | collective-permute-start | bytes 393224 | tf_op jit(solution)/shard_map/ppermute | solution.py:445
  118.1 1.5 %collective-permute-start.30 = (bf16[512,128]{1,0:T(8,128)(2,1)S(1)}, bf16[512,128]{1,0:T(8,128)(2,1)S(1)}, u32[]{:S(2)}, u32[]{:S(2)}) collective-permute-start(bf16[512,128]{1,0:T(8,128)(2,1)S(1)} %get-tuple-element.112), channel_id=1, source_target_pairs={{0,4},{4,0},{8,12},{12,8},{16,20},{20,16},{24,28},{28,24},{1,5},{5... | collective-permute-start | bytes 393224 | tf_op jit(solution)/shard_map/ppermute | solution.py:445
  119.6 6.8 %shard_map.112 = (bf16[2048,512]{1,0:T(8,128)(2,1)}, f32[1024,512]{1,0:T(8,128)S(1)}, f32[1024,512]{1,0:T(8,128)S(1)}) custom-call(s32[65]{0:T(128)S(1)} %copy-done.5, s32[8]{0:T(128)S(1)} %copy-done.4, f32[4]{0:T(128)S(1)} %copy-done.3, f32[8,256]{1,0:T(8,128)S(1)} %get-tuple-element.64.refs_8_.seg_ref, ...), custom_call_target="tpu_custom_call", output_to_operand_aliasing={{0}: (16, {})} | custom-call | flops 1610612736 | tf_op jit(solution)/shard_map/pallas_call | solution.py:605
  126.5 3.8 %shard_map.114 = (bf16[2048,512]{1,0:T(8,128)(2,1)}, bf16[2048,512]{1,0:T(8,128)(2,1)}) custom-call(s32[65]{0:T(128)S(1)} %copy-done.7, s32[8]{0:T(128)S(1)} %copy-done.4, f32[4]{0:T(128)S(1)} %copy-done.3, bf16[2048,512]{1,0:T(8,128)(2,1)S(1)} %get-tuple-element.62.k_ref, bf16[2048,512]{1,0:T(8,128)(2,1)S(1)} %get-tuple-element.63.v_ref, ...), custom_call_target="tpu_custom_call" | custom-call | flops 268435456 | tf_op jit(solution)/shard_map/pallas_call | solution.py:622
  130.3 2.1 %shard_map.115 = (bf16[2048,512]{1,0:T(8,128)(2,1)}, bf16[2048,512]{1,0:T(8,128)(2,1)}) custom-call(s32[65]{0:T(128)S(1)} %copy-done.7, s32[8]{0:T(128)S(1)} %copy-done.4, f32[4]{0:T(128)S(1)} %copy-done.3, bf16[2048,512]{1,0:T(8,128)(2,1)S(1)} %get-tuple-element.62.k_ref, ...), custom_call_target="tpu_custom_call", output_to_operand_aliasing={{0}: (11, {}), {1}: (12, {})} | custom-call | flops 268435456 | tf_op jit(solution)/shard_map/pallas_call | solution.py:622
  (45 shorter events, 1.4 us)
Async XLA Ops:
  3.8 14.4 %collective-permute-start.5 = (bf16[528,128]{1,0:T(8,128)(2,1)}, bf16[528,128]{1,0:T(8,128)(2,1)S(1)}, u32[]{:S(2)}, u32[]{:S(2)}) collective-permute-start(bf16[528,128]{1,0:T(8,128)(2,1)} %get-tuple-element.74), channel_id=1, source_target_pairs={{0,24},{4,28},{8,16},{12,20},{16,8},{20,12},{24,0},{28,4},{1,25},{... | collective-permute-start | bytes 405512 | tf_op jit(solution)/shard_map/ppermute | solution.py:445
  9.0 11.5 %collective-permute-start.6 = (bf16[528,128]{1,0:T(8,128)(2,1)}, bf16[528,128]{1,0:T(8,128)(2,1)S(1)}, u32[]{:S(2)}, u32[]{:S(2)}) collective-permute-start(bf16[528,128]{1,0:T(8,128)(2,1)} %get-tuple-element.75), channel_id=1, source_target_pairs={{0,28},{4,24},{8,20},{12,16},{16,12},{20,8},{24,4},{28,0},{1,29},{... | collective-permute-start | bytes 405512 | tf_op jit(solution)/shard_map/ppermute | solution.py:445
  10.2 13.2 %copy-start.3 = (f32[4]{0:T(128)S(1)}, f32[4]{0:T(128)}, u32[]{:S(2)}) copy-start(f32[4]{0:T(128)} %rate_ref.21) | copy-start | bytes 52
  10.2 13.2 %copy-start.4 = (s32[8]{0:T(128)S(1)}, s32[8]{0:T(128)}, u32[]{:S(2)}) copy-start(s32[8]{0:T(128)} %home_ref.17) | copy-start | bytes 100
  10.2 13.2 %copy-start.8 = (s32[32]{0:T(128)S(1)}, s32[32]{0:T(128)}, u32[]{:S(2)}) copy-start(s32[32]{0:T(128)} %len_ref.1) | copy-start | bytes 388
  14.7 16.1 %collective-permute-start = (bf16[528,128]{1,0:T(8,128)(2,1)}, bf16[528,128]{1,0:T(8,128)(2,1)S(1)}, u32[]{:S(2)}, u32[]{:S(2)}) collective-permute-start(bf16[528,128]{1,0:T(8,128)(2,1)} %get-tuple-element.69), channel_id=1, source_target_pairs={{0,4},{4,0},{8,12},{12,8},{16,20},{20,16},{24,28},{28,24},{1,5},{5... | collective-permute-start | bytes 405512 | tf_op jit(solution)/shard_map/ppermute | solution.py:445
  15.1 15.7 %collective-permute-start.1 = (bf16[528,128]{1,0:T(8,128)(2,1)}, bf16[528,128]{1,0:T(8,128)(2,1)S(1)}, u32[]{:S(2)}, u32[]{:S(2)}) collective-permute-start(bf16[528,128]{1,0:T(8,128)(2,1)} %get-tuple-element.70), channel_id=1, source_target_pairs={{0,8},{4,12},{8,0},{12,4},{16,24},{20,28},{24,16},{28,20},{1,9},{5... | collective-permute-start | bytes 405512 | tf_op jit(solution)/shard_map/ppermute | solution.py:445
  15.1 15.7 %collective-permute-start.2 = (bf16[528,128]{1,0:T(8,128)(2,1)}, bf16[528,128]{1,0:T(8,128)(2,1)S(1)}, u32[]{:S(2)}, u32[]{:S(2)}) collective-permute-start(bf16[528,128]{1,0:T(8,128)(2,1)} %get-tuple-element.71), channel_id=1, source_target_pairs={{0,12},{4,8},{8,4},{12,0},{16,28},{20,24},{24,20},{28,16},{1,13},{... | collective-permute-start | bytes 405512 | tf_op jit(solution)/shard_map/ppermute | solution.py:445
  18.3 13.1 %collective-permute-start.3 = (bf16[528,128]{1,0:T(8,128)(2,1)}, bf16[528,128]{1,0:T(8,128)(2,1)S(1)}, u32[]{:S(2)}, u32[]{:S(2)}) collective-permute-start(bf16[528,128]{1,0:T(8,128)(2,1)} %get-tuple-element.72), channel_id=1, source_target_pairs={{0,16},{4,20},{8,24},{12,28},{16,0},{20,4},{24,8},{28,12},{1,17},{... | collective-permute-start | bytes 405512 | tf_op jit(solution)/shard_map/ppermute | solution.py:445
  20.5 12.9 %collective-permute-start.4 = (bf16[528,128]{1,0:T(8,128)(2,1)}, bf16[528,128]{1,0:T(8,128)(2,1)S(1)}, u32[]{:S(2)}, u32[]{:S(2)}) collective-permute-start(bf16[528,128]{1,0:T(8,128)(2,1)} %get-tuple-element.73), channel_id=1, source_target_pairs={{0,20},{4,16},{8,28},{12,24},{16,4},{20,0},{24,12},{28,8},{1,21},{... | collective-permute-start | bytes 405512 | tf_op jit(solution)/shard_map/ppermute | solution.py:445
  23.3 1.6 %copy-start = (bf16[2048,512]{1,0:T(8,128)(2,1)S(1)}, bf16[2048,512]{1,0:T(8,128)(2,1)}, u32[]{:S(2)}) copy-start(bf16[2048,512]{1,0:T(8,128)(2,1)} %q_hbm.1) | copy-start | bytes 6291460
  24.9 1.6 %copy-start.1 = (bf16[2048,512]{1,0:T(8,128)(2,1)S(1)}, bf16[2048,512]{1,0:T(8,128)(2,1)}, u32[]{:S(2)}) copy-start(bf16[2048,512]{1,0:T(8,128)(2,1)} %u_hbm.1) | copy-start | bytes 6291460
  26.5 6.8 %copy-start.2 = (bf16[528,128]{1,0:T(8,128)(2,1)S(1)}, bf16[528,128]{1,0:T(8,128)(2,1)}, u32[]{:S(2)}) copy-start(bf16[528,128]{1,0:T(8,128)(2,1)} %get-tuple-element.68.refs_0_) | copy-start | bytes 405508
  26.5 6.8 %copy-start.5 = (s32[65]{0:T(128)S(1)}, s32[65]{0:T(128)}, u32[]{:S(2)}) copy-start(s32[65]{0:T(128)} %get-tuple-element.60.first_ref) | copy-start | bytes 784
  26.5 28.9 %copy-start.6 = (f32[512]{0:T(512)S(1)}, f32[512]{0:T(512)}, u32[]{:S(2)}) copy-start(f32[512]{0:T(512)} %param.12) | copy-start | bytes 6148
  35.6 8.0 %collective-permute-start.9 = (bf16[512,128]{1,0:T(8,128)(2,1)S(1)}, bf16[512,128]{1,0:T(8,128)(2,1)S(1)}, u32[]{:S(2)}, u32[]{:S(2)}) collective-permute-start(bf16[512,128]{1,0:T(8,128)(2,1)S(1)} %get-tuple-element.78), channel_id=1, source_target_pairs={{0,24},{4,28},{8,16},{12,20},{16,8},{20,12},{24,0},{28,4},{1,25},{... | collective-permute-start | bytes 393224 | tf_op jit(solution)/shard_map/ppermute | solution.py:445
  38.1 9.1 %collective-permute-start.10 = (bf16[512,128]{1,0:T(8,128)(2,1)S(1)}, bf16[512,128]{1,0:T(8,128)(2,1)S(1)}, u32[]{:S(2)}, u32[]{:S(2)}) collective-permute-start(bf16[512,128]{1,0:T(8,128)(2,1)S(1)} %get-tuple-element.79), channel_id=1, source_target_pairs={{0,28},{4,24},{8,20},{12,16},{16,12},{20,8},{24,4},{28,0},{1,29},{... | collective-permute-start | bytes 393224 | tf_op jit(solution)/shard_map/ppermute | solution.py:445
  40.1 11.2 %collective-permute-start.11 = (bf16[512,128]{1,0:T(8,128)(2,1)S(1)}, bf16[512,128]{1,0:T(8,128)(2,1)S(1)}, u32[]{:S(2)}, u32[]{:S(2)}) collective-permute-start(bf16[512,128]{1,0:T(8,128)(2,1)S(1)} %get-tuple-element.80), channel_id=1, source_target_pairs={{0,8},{4,12},{8,0},{12,4},{16,24},{20,28},{24,16},{28,20},{1,9},{5... | collective-permute-start | bytes 393224 | tf_op jit(solution)/shard_map/ppermute | solution.py:445
  40.1 15.3 %collective-permute-start.12 = (bf16[512,128]{1,0:T(8,128)(2,1)S(1)}, bf16[512,128]{1,0:T(8,128)(2,1)S(1)}, u32[]{:S(2)}, u32[]{:S(2)}) collective-permute-start(bf16[512,128]{1,0:T(8,128)(2,1)S(1)} %get-tuple-element.81), channel_id=1, source_target_pairs={{0,12},{4,8},{8,4},{12,0},{16,28},{20,24},{24,20},{28,16},{1,13},{... | collective-permute-start | bytes 393224 | tf_op jit(solution)/shard_map/ppermute | solution.py:445
  42.4 13.1 %collective-permute-start.13 = (bf16[512,128]{1,0:T(8,128)(2,1)S(1)}, bf16[512,128]{1,0:T(8,128)(2,1)S(1)}, u32[]{:S(2)}, u32[]{:S(2)}) collective-permute-start(bf16[512,128]{1,0:T(8,128)(2,1)S(1)} %get-tuple-element.83), channel_id=1, source_target_pairs={{0,4},{4,0},{8,12},{12,8},{16,20},{20,16},{24,28},{28,24},{1,5},{5... | collective-permute-start | bytes 393224 | tf_op jit(solution)/shard_map/ppermute | solution.py:445
  43.6 14.3 %collective-permute-start.7 = (bf16[512,128]{1,0:T(8,128)(2,1)S(1)}, bf16[512,128]{1,0:T(8,128)(2,1)S(1)}, u32[]{:S(2)}, u32[]{:S(2)}) collective-permute-start(bf16[512,128]{1,0:T(8,128)(2,1)S(1)} %get-tuple-element.76), channel_id=1, source_target_pairs={{0,16},{4,20},{8,24},{12,28},{16,0},{20,4},{24,8},{28,12},{1,17},{... | collective-permute-start | bytes 393224 | tf_op jit(solution)/shard_map/ppermute | solution.py:445
  47.1 11.5 %collective-permute-start.8 = (bf16[512,128]{1,0:T(8,128)(2,1)S(1)}, bf16[512,128]{1,0:T(8,128)(2,1)S(1)}, u32[]{:S(2)}, u32[]{:S(2)}) collective-permute-start(bf16[512,128]{1,0:T(8,128)(2,1)S(1)} %get-tuple-element.77), channel_id=1, source_target_pairs={{0,20},{4,16},{8,28},{12,24},{16,4},{20,0},{24,12},{28,8},{1,21},{... | collective-permute-start | bytes 393224 | tf_op jit(solution)/shard_map/ppermute | solution.py:445
  60.0 1.9 %collective-permute-start.16 = (f32[2,8,256]{2,1,0:T(8,128)S(1)}, f32[2,8,256]{2,1,0:T(8,128)S(1)}, u32[]{:S(2)}, u32[]{:S(2)}) collective-permute-start(f32[2,8,256]{2,1,0:T(8,128)S(1)} %get-tuple-element.87.refs_3_), channel_id=1, source_target_pairs={{0,1},{1,0},{2,3},{3,2},{4,5},{5,4},{6,7},{7,6},{8,9},{9,8},{10,11... | collective-permute-start | bytes 49160 | tf_op jit(solution)/shard_map/ppermute | solution.py:445
  60.1 3.8 %collective-permute-start.15 = (f32[2,8,256]{2,1,0:T(8,128)S(1)}, f32[2,8,256]{2,1,0:T(8,128)S(1)}, u32[]{:S(2)}, u32[]{:S(2)}) collective-permute-start(f32[2,8,256]{2,1,0:T(8,128)S(1)} %get-tuple-element.87.refs_3_), channel_id=1, source_target_pairs={{0,2},{1,3},{2,0},{3,1},{4,6},{5,7},{6,4},{7,5},{8,10},{9,11},{10,... | collective-permute-start | bytes 49160 | tf_op jit(solution)/shard_map/ppermute | solution.py:445
  61.7 3.2 %collective-permute-start.14 = (f32[2,8,256]{2,1,0:T(8,128)S(1)}, f32[2,8,256]{2,1,0:T(8,128)S(1)}, u32[]{:S(2)}, u32[]{:S(2)}) collective-permute-start(f32[2,8,256]{2,1,0:T(8,128)S(1)} %get-tuple-element.87.refs_3_), channel_id=1, source_target_pairs={{0,3},{1,2},{2,1},{3,0},{4,7},{5,6},{6,5},{7,4},{8,11},{9,10},{10,... | collective-permute-start | bytes 49160 | tf_op jit(solution)/shard_map/ppermute | solution.py:445
  69.1 7.2 %collective-permute-start.17 = (bf16[512,128]{1,0:T(8,128)(2,1)S(1)}, bf16[512,128]{1,0:T(8,128)(2,1)S(1)}, u32[]{:S(2)}, u32[]{:S(2)}) collective-permute-start(bf16[512,128]{1,0:T(8,128)(2,1)S(1)} %get-tuple-element.98), channel_id=1, source_target_pairs={{0,4},{4,0},{8,12},{12,8},{16,20},{20,16},{24,28},{28,24},{1,5},{5... | collective-permute-start | bytes 393224 | tf_op jit(solution)/shard_map/ppermute | solution.py:445
  70.5 9.2 %collective-permute-start.18 = (bf16[512,128]{1,0:T(8,128)(2,1)S(1)}, bf16[512,128]{1,0:T(8,128)(2,1)S(1)}, u32[]{:S(2)}, u32[]{:S(2)}) collective-permute-start(bf16[512,128]{1,0:T(8,128)(2,1)S(1)} %get-tuple-element.99), channel_id=1, source_target_pairs={{0,8},{4,12},{8,0},{12,4},{16,24},{20,28},{24,16},{28,20},{1,9},{5... | collective-permute-start | bytes 393224 | tf_op jit(solution)/shard_map/ppermute | solution.py:445
  70.5 11.6 %collective-permute-start.19 = (bf16[512,128]{1,0:T(8,128)(2,1)S(1)}, bf16[512,128]{1,0:T(8,128)(2,1)S(1)}, u32[]{:S(2)}, u32[]{:S(2)}) collective-permute-start(bf16[512,128]{1,0:T(8,128)(2,1)S(1)} %get-tuple-element.100), channel_id=1, source_target_pairs={{0,12},{4,8},{8,4},{12,0},{16,28},{20,24},{24,20},{28,16},{1,13},{... | collective-permute-start | bytes 393224 | tf_op jit(solution)/shard_map/ppermute | solution.py:445
  72.7 18.5 %collective-permute-start.20 = (bf16[512,128]{1,0:T(8,128)(2,1)S(1)}, bf16[512,128]{1,0:T(8,128)(2,1)S(1)}, u32[]{:S(2)}, u32[]{:S(2)}) collective-permute-start(bf16[512,128]{1,0:T(8,128)(2,1)S(1)} %get-tuple-element.101), channel_id=1, source_target_pairs={{0,16},{4,20},{8,24},{12,28},{16,0},{20,4},{24,8},{28,12},{1,17},{... | collective-permute-start | bytes 393224 | tf_op jit(solution)/shard_map/ppermute | solution.py:445
  73.1 21.6 %collective-permute-start.21 = (bf16[512,128]{1,0:T(8,128)(2,1)S(1)}, bf16[512,128]{1,0:T(8,128)(2,1)S(1)}, u32[]{:S(2)}, u32[]{:S(2)}) collective-permute-start(bf16[512,128]{1,0:T(8,128)(2,1)S(1)} %get-tuple-element.102), channel_id=1, source_target_pairs={{0,20},{4,16},{8,28},{12,24},{16,4},{20,0},{24,12},{28,8},{1,21},{... | collective-permute-start | bytes 393224 | tf_op jit(solution)/shard_map/ppermute | solution.py:445
  76.4 18.4 %collective-permute-start.22 = (bf16[512,128]{1,0:T(8,128)(2,1)S(1)}, bf16[512,128]{1,0:T(8,128)(2,1)S(1)}, u32[]{:S(2)}, u32[]{:S(2)}) collective-permute-start(bf16[512,128]{1,0:T(8,128)(2,1)S(1)} %get-tuple-element.103), channel_id=1, source_target_pairs={{0,24},{4,28},{8,16},{12,20},{16,8},{20,12},{24,0},{28,4},{1,25},{... | collective-permute-start | bytes 393224 | tf_op jit(solution)/shard_map/ppermute | solution.py:445
  79.7 15.0 %collective-permute-start.23 = (bf16[512,128]{1,0:T(8,128)(2,1)S(1)}, bf16[512,128]{1,0:T(8,128)(2,1)S(1)}, u32[]{:S(2)}, u32[]{:S(2)}) collective-permute-start(bf16[512,128]{1,0:T(8,128)(2,1)S(1)} %get-tuple-element.104), channel_id=1, source_target_pairs={{0,28},{4,24},{8,20},{12,16},{16,12},{20,8},{24,4},{28,0},{1,29},{... | collective-permute-start | bytes 393224 | tf_op jit(solution)/shard_map/ppermute | solution.py:445
  96.0 22.1 %collective-permute-start.26 = (bf16[512,128]{1,0:T(8,128)(2,1)S(1)}, bf16[512,128]{1,0:T(8,128)(2,1)S(1)}, u32[]{:S(2)}, u32[]{:S(2)}) collective-permute-start(bf16[512,128]{1,0:T(8,128)(2,1)S(1)} %get-tuple-element.107), channel_id=1, source_target_pairs={{0,24},{4,28},{8,16},{12,20},{16,8},{20,12},{24,0},{28,4},{1,25},{... | collective-permute-start | bytes 393224 | tf_op jit(solution)/shard_map/ppermute | solution.py:445
  97.5 20.6 %collective-permute-start.27 = (bf16[512,128]{1,0:T(8,128)(2,1)S(1)}, bf16[512,128]{1,0:T(8,128)(2,1)S(1)}, u32[]{:S(2)}, u32[]{:S(2)}) collective-permute-start(bf16[512,128]{1,0:T(8,128)(2,1)S(1)} %get-tuple-element.108), channel_id=1, source_target_pairs={{0,28},{4,24},{8,20},{12,16},{16,12},{20,8},{24,4},{28,0},{1,29},{... | collective-permute-start | bytes 393224 | tf_op jit(solution)/shard_map/ppermute | solution.py:445
  106.9 23.4 %collective-permute-start.24 = (bf16[512,128]{1,0:T(8,128)(2,1)S(1)}, bf16[512,128]{1,0:T(8,128)(2,1)S(1)}, u32[]{:S(2)}, u32[]{:S(2)}) collective-permute-start(bf16[512,128]{1,0:T(8,128)(2,1)S(1)} %get-tuple-element.105), channel_id=1, source_target_pairs={{0,16},{4,20},{8,24},{12,28},{16,0},{20,4},{24,8},{28,12},{1,17},{... | collective-permute-start | bytes 393224 | tf_op jit(solution)/shard_map/ppermute | solution.py:445
  114.7 15.6 %collective-permute-start.25 = (bf16[512,128]{1,0:T(8,128)(2,1)S(1)}, bf16[512,128]{1,0:T(8,128)(2,1)S(1)}, u32[]{:S(2)}, u32[]{:S(2)}) collective-permute-start(bf16[512,128]{1,0:T(8,128)(2,1)S(1)} %get-tuple-element.106), channel_id=1, source_target_pairs={{0,20},{4,16},{8,28},{12,24},{16,4},{20,0},{24,12},{28,8},{1,21},{... | collective-permute-start | bytes 393224 | tf_op jit(solution)/shard_map/ppermute | solution.py:445
  114.8 11.7 %collective-permute-start.28 = (bf16[512,128]{1,0:T(8,128)(2,1)S(1)}, bf16[512,128]{1,0:T(8,128)(2,1)S(1)}, u32[]{:S(2)}, u32[]{:S(2)}) collective-permute-start(bf16[512,128]{1,0:T(8,128)(2,1)S(1)} %get-tuple-element.109), channel_id=1, source_target_pairs={{0,8},{4,12},{8,0},{12,4},{16,24},{20,28},{24,16},{28,20},{1,9},{5... | collective-permute-start | bytes 393224 | tf_op jit(solution)/shard_map/ppermute | solution.py:445
  118.1 8.3 %collective-permute-start.29 = (bf16[512,128]{1,0:T(8,128)(2,1)S(1)}, bf16[512,128]{1,0:T(8,128)(2,1)S(1)}, u32[]{:S(2)}, u32[]{:S(2)}) collective-permute-start(bf16[512,128]{1,0:T(8,128)(2,1)S(1)} %get-tuple-element.110), channel_id=1, source_target_pairs={{0,12},{4,8},{8,4},{12,0},{16,28},{20,24},{24,20},{28,16},{1,13},{... | collective-permute-start | bytes 393224 | tf_op jit(solution)/shard_map/ppermute | solution.py:445
  118.1 8.3 %collective-permute-start.30 = (bf16[512,128]{1,0:T(8,128)(2,1)S(1)}, bf16[512,128]{1,0:T(8,128)(2,1)S(1)}, u32[]{:S(2)}, u32[]{:S(2)}) collective-permute-start(bf16[512,128]{1,0:T(8,128)(2,1)S(1)} %get-tuple-element.112), channel_id=1, source_target_pairs={{0,4},{4,0},{8,12},{12,8},{16,20},{20,16},{24,28},{28,24},{1,5},{5... | collective-permute-start | bytes 393224 | tf_op jit(solution)/shard_map/ppermute | solution.py:445
  119.6 6.9 %copy-start.7 = (s32[65]{0:T(128)S(1)}, s32[65]{0:T(128)}, u32[]{:S(2)}) copy-start(s32[65]{0:T(128)} %get-tuple-element.61.refs_0_.last_ref) | copy-start | bytes 784

commit v2 on v1

--- a/solution.py
+++ b/solution.py
@@ -267,7 +267,7 @@
 
 def local_kernel(
     heads, span, len_ref, home_ref, rate_ref, q_hbm, u_hbm, k_ref, v_ref,
-    out_ref, q_ref, u_ref, seg_ref, decay, sem, u_sem,
+    out_ref, q_ref, u_ref, seg_ref, side_ref, decay, sem, u_sem,
 ):
     slots = home_ref.shape[0]
     load = lambda i: span_copies(i, span, (q_hbm,), (q_ref,), sem)
@@ -277,6 +277,8 @@
     for i in range(slots):
         start_all(later(i))
     fill_segments(seg_ref, len_ref, home_ref)
+    for h in range(heads):
+        side_ref[h] = query_side(rate_ref[h], span)
     fill_decay(decay, rate_ref, 0, span)
 
     def body(i):
@@ -295,18 +297,16 @@
 
 
 def output_kernel(
-    groups, rows, span, count, again, first_ref, home_ref, rate_ref, gain_ref, q_ref, u_ref, inner_ref, *refs
+    groups, rows, span, count, again, first_ref, home_ref, side_ref, gain_ref, q_ref, u_ref, inner_ref, *refs
 ):
     blocks, refs = refs[:count], refs[count:]
     if again:
         before_ref, refs = refs[0], refs[2:]
-    out_ref, sums_ref, prev, table = refs
+    out_ref, sums_ref, prev = refs
     slots = home_ref.shape[0]
     chunks = HEAD_SIZE // rows
     heads = [group_head(p, chunks) for p in groups]
     take_groups(blocks, prev, chunks)
-    for g, (head, cols) in enumerate(heads):
-        table[g] = query_side(rate_ref[head], span)
 
     def body(i):
         at = tokens_at(i, span)
@@ -315,7 +315,7 @@
         crossed = jnp.zeros((span, LANES), F32)
         for g, (head, cols) in enumerate(heads):
             outer = dot(q_ref[at, cols], get_group(prev, g, i, rows), 1, 0)
-            attn = inner_ref[at, cols] + jnp.where(live, table[g], 0.0) * outer
+            attn = inner_ref[at, cols] + jnp.where(live, side_ref[head], 0.0) * outer
             out_ref[at, cols] = attn
             squares += attn * attn
             crossed += gain_ref[:, cols] * u_ref[at, cols].astype(F32) * attn
@@ -330,11 +330,11 @@
 
 
 def cotangent_kernel(
-    groups, rows, span, count, again, channels, others, first_ref, home_ref, rate_ref, gain_ref, q_ref, u_ref, attn_ref, *refs
+    groups, rows, span, count, again, channels, others, first_ref, home_ref, side_ref, gain_ref, q_ref, u_ref, attn_ref, *refs
 ):
     sums, refs = refs[:others], refs[others + again :]
     g_ref, blocks = refs[0], refs[1 : 1 + count]
-    table, factors, packed = refs[1 + count :]
+    factors, packed = refs[1 + count :]
     slots = home_ref.shape[0]
     chunks = HEAD_SIZE // rows
     heads = [group_head(p, chunks) for p in groups]
@@ -342,8 +342,6 @@
     pulled = sum(ref[1] for ref in sums) / channels
     factors[0] = scaling
     factors[1] = scaling * scaling * scaling * pulled
-    for g, (head, cols) in enumerate(heads):
-        table[g] = query_side(rate_ref[head], span)
 
     def body(i):
         at = tokens_at(i, span)
@@ -354,7 +352,7 @@
             grad = direct * gain_ref[:, cols] * u_ref[at, cols].astype(F32)
             grad = (grad - along * attn_ref[at, cols]).astype(BF16)
             g_ref[at, cols] = grad
-            weighted = (jnp.where(live, table[g], 0.0) * grad.astype(F32)).astype(BF16)
+            weighted = (jnp.where(live, side_ref[head], 0.0) * grad.astype(F32)).astype(BF16)
             put_group(packed, g, i, rows, dot(q_ref[at, cols], weighted, 0, 0).astype(BF16))
 
     each_span(slots, UNROLL["cotangent"], nothing, body, nothing)
@@ -534,11 +532,11 @@
     moving.update(zip(masks_of(behind), sent))
     arrived = exchange(moving)
 
-    inner, query_v, upstream_v, seg = call(
+    inner, query_v, upstream_v, seg, side = call(
         local_kernel, LIMIT, 2 * work,
         [smem, smem, smem, hbm, hbm, vmem, vmem],
-        [vmem, vmem, vmem, vmem],
-        [token_f32, token_bf16, token_bf16, pltpu.VMEM((slots, span), F32)],
+        [vmem] * 5,
+        [token_f32, token_bf16, token_bf16, pltpu.VMEM((slots, span), F32), table],
         [decay, sems(1, slots), sems(1, slots)],
         heads, span,
     )(document_lengths, group_home, decay_rate, query, upstream, key_v, value_v)
@@ -568,13 +566,13 @@
         again = len(before) > 0
         return call(
             output_kernel, LIMIT, work // 4,
-            [smem, smem, smem] + [vmem] * (4 + count + len(before)),
+            [smem, smem, vmem] + [vmem] * (4 + count + len(before)),
             [vmem, vmem],
             [token_f32, jax.ShapeDtypeStruct((2, slots, span), F32)],
-            [states_of(groups), table_of(groups)],
+            [states_of(groups)],
             groups, rows, span, count, again,
             aliases={8 + count: 0} if again else {},
-        )(first, group_home, decay_rate, gain, query_v, upstream_v, inner, *pick(prev, groups), *before)
+        )(first, group_home, side, gain, query_v, upstream_v, inner, *pick(prev, groups), *before)
 
     attn, sums = outputs(early)
     attn, sums = outputs(late, sums, attn)
@@ -585,13 +583,13 @@
         others = len(sums)
         return call(
             cotangent_kernel, LIMIT, work // 4,
-            [smem, smem, smem] + [vmem] * (4 + others + len(before)),
+            [smem, smem, vmem] + [vmem] * (4 + others + len(before)),
             [vmem] * (1 + count),
             [token_bf16] + out[:count],
-            [table_of(groups), pltpu.VMEM((2, slots, span), F32), states_of(groups)],
+            [pltpu.VMEM((2, slots, span), F32), states_of(groups)],
             groups, rows, span, count, len(before), channels, others,
             aliases={7 + others: 0} if before else {},
-        )(first, group_home, decay_rate, gain, query_v, upstream_v, attn, *sums, *before)
+        )(first, group_home, side, gain, query_v, upstream_v, attn, *sums, *before)
 
     grad_in, *sent = cotangents(ahead)
     moving = dict(zip(masks_of(ahead), sent))

time: 133 us -> 133 us (level)
  no operation moved by 1% of the time
where the time goes in v2:
time: 133 us
  starting transfers between devices  56 us (42%)
  Pallas kernels  43.5 us (33%)
  waiting for transfers between devices  29 us (22%)
  local copies, waits for them, and re-layouts  3.2 us (2%)
    ppermute x31, starting transfers between devices, swap(): lax.ppermute(array, axis, [(i, i ^ mask) for i in range(lax.axis_size(axi...  56 us
    ppermute x31, waiting for transfers between devices, swap(): lax.ppermute(array, axis, [(i, i ^ mask) for i in range(lax.axis_size(axi...  29 us
    pallas_call x2, Pallas kernels, inner_grads(): call(inner_grads_kernel, LIMIT, 3 * work, [smem, smem, smem, vmem, vmem,...  13.7 us
    pallas_call x2, Pallas kernels, outer_grads(): call(outer_grads_kernel, LIMIT, work // 2, [smem, smem, smem] + [vmem] *...  5.84 us
    pallas_call x1, Pallas kernels, shards(): call(summary_kernel, ALONE, work // 2, [smem, smem, smem, hbm, hbm], [vme...  4.53 us
    pallas_call x2, Pallas kernels, cotangents(): call(cotangent_kernel, LIMIT, work // 4, [smem, smem, vmem] + [vmem] * (4...  4.48 us
    pallas_call x1, Pallas kernels, shards(): call(local_kernel, LIMIT, 2 * work, [smem, smem, smem, hbm, hbm, vmem, vm...  4.39 us
    pallas_call x2, Pallas kernels, outputs(): call(output_kernel, LIMIT, work // 4, [smem, smem, vmem] + [vmem] * (4 +...  3.96 us
  transfers between devices with their start and end apart: 31, of which 11 were waited for; matrix products, arithmetic and copies ran while one was open for 0% of the time, Pallas kernels for 22%

profile of v2, /device:TPU:0, one launch (start us, length us, event | category | flops | bytes accessed | tf_op | source)
XLA Modules:
  0.0 132.7 jit_solution(15295768506285430262)
XLA Ops:
  0.6 3.2 %shard_map.103 = (bf16[528,128]{1,0:T(8,128)(2,1)}, bf16[528,128]{1,0:T(8,128)(2,1)}, s32[65]{0:T(128)}, s32[65]{0:T(128)}) custom-call(s32[32]{0:T(128)} %len_ref.1, s32[8]{0:T(128)} %home_ref.17, f32[4]{0:T(128)} %rate_ref.13, bf16[2048,512]{1,0:T(8,128)(2,1)} %refs_3_.3, bf16[2048,512]{1,0:T(8,128)(2,1)} %refs_4_.3), custom_call_target="tpu_custom_call" | custom-call | flops 67108864 | tf_op jit(solution)/shard_map/pallas_call | solution.py:514
  3.8 5.1 %collective-permute-start.5 = (bf16[528,128]{1,0:T(8,128)(2,1)}, bf16[528,128]{1,0:T(8,128)(2,1)S(1)}, u32[]{:S(2)}, u32[]{:S(2)}) collective-permute-start(bf16[528,128]{1,0:T(8,128)(2,1)} %get-tuple-element.76), channel_id=1, source_target_pairs={{0,24},{4,28},{8,16},{12,20},{16,8},{20,12},{24,0},{28,4},{1,25},{... | collective-permute-start | bytes 405512 | tf_op jit(solution)/shard_map/ppermute | solution.py:443
  9.0 1.2 collective-permute-start.6
  10.2 4.5 %shard_map.104 = (bf16[528,128]{1,0:T(8,128)(2,1)}, bf16[528,128]{1,0:T(8,128)(2,1)}, bf16[528,128]{1,0:T(8,128)(2,1)}, bf16[528,128]{1,0:T(8,128)(2,1)}, bf16[5...) custom-call(s32[65]{0:T(128)} %get-tuple-element.62.refs_0_.last_ref, ...), custom_call_target="tpu_custom_call" | custom-call | flops 268435456 | tf_op jit(solution)/shard_map/pallas_call | solution.py:524
  14.7 0.4 collective-permute-start
  15.1 3.1 %collective-permute-start.2 = (bf16[528,128]{1,0:T(8,128)(2,1)}, bf16[528,128]{1,0:T(8,128)(2,1)S(1)}, u32[]{:S(2)}, u32[]{:S(2)}) collective-permute-start(bf16[528,128]{1,0:T(8,128)(2,1)} %get-tuple-element.73), channel_id=1, source_target_pairs={{0,12},{4,8},{8,4},{12,0},{16,28},{20,24},{24,20},{28,16},{1,13},{... | collective-permute-start | bytes 405512 | tf_op jit(solution)/shard_map/ppermute | solution.py:443
  18.3 2.2 %collective-permute-start.3 = (bf16[528,128]{1,0:T(8,128)(2,1)}, bf16[528,128]{1,0:T(8,128)(2,1)S(1)}, u32[]{:S(2)}, u32[]{:S(2)}) collective-permute-start(bf16[528,128]{1,0:T(8,128)(2,1)} %get-tuple-element.74), channel_id=1, source_target_pairs={{0,16},{4,20},{8,24},{12,28},{16,0},{20,4},{24,8},{28,12},{1,17},{... | collective-permute-start | bytes 405512 | tf_op jit(solution)/shard_map/ppermute | solution.py:443
  20.5 2.9 %collective-permute-start.4 = (bf16[528,128]{1,0:T(8,128)(2,1)}, bf16[528,128]{1,0:T(8,128)(2,1)S(1)}, u32[]{:S(2)}, u32[]{:S(2)}) collective-permute-start(bf16[528,128]{1,0:T(8,128)(2,1)} %get-tuple-element.75), channel_id=1, source_target_pairs={{0,20},{4,16},{8,28},{12,24},{16,4},{20,0},{24,12},{28,8},{1,21},{... | collective-permute-start | bytes 405512 | tf_op jit(solution)/shard_map/ppermute | solution.py:443
  23.3 1.6 %copy-done = bf16[2048,512]{1,0:T(8,128)(2,1)S(1)} copy-done((bf16[2048,512]{1,0:T(8,128)(2,1)S(1)}, bf16[2048,512]{1,0:T(8,128)(2,1)}, u32[]{:S(2)}) %copy-start) | copy-done | bytes 2097176
  24.9 1.6 %copy-done.1 = bf16[2048,512]{1,0:T(8,128)(2,1)S(1)} copy-done((bf16[2048,512]{1,0:T(8,128)(2,1)S(1)}, bf16[2048,512]{1,0:T(8,128)(2,1)}, u32[]{:S(2)}) %copy-start.1) | copy-done | bytes 2097176
  26.5 4.4 %shard_map.105 = (f32[2048,512]{1,0:T(8,128)S(1)}, bf16[2048,512]{1,0:T(8,128)(2,1)S(1)}, bf16[2048,512]{1,0:T(8,128)(2,1)S(1)}, f32[8,256]{1,0:T(8,128)S(1)}, f32[4,256,128]{2,1,0:T(8,128)S(1)}) custom-call(s32[32]{0:T(128)S(1)} %copy-done.8, s32[8]{0:T(128)S(1)} %copy-done.3, f32[4]{0:T(128)S(1)} %copy-done.4, bf16[2048,512]{1,0:T(8,128)(2,1)S(1)} %copy-done, ...), custom_call_target="tpu_custom_call" | custom-call | flops 1073741824 | tf_op jit(solution)/shard_map/pallas_call | solution.py:535
  31.4 2.0 %collective-permute-done.4.refs_5_ = bf16[528,128]{1,0:T(8,128)(2,1)S(1)} collective-permute-done((bf16[528,128]{1,0:T(8,128)(2,1)}, bf16[528,128]{1,0:T(8,128)(2,1)S(1)}, u32[]{:S(2)}, u32[]{:S(2)}) %collective-permute-start.4) | collective-permute-done | bytes 135200 | tf_op jit(solution)/shard_map/ppermute | solution.py:443
  33.3 2.2 %shard_map.106 = (bf16[512,128]{1,0:T(8,128)(2,1)S(1)}, bf16[512,128]{1,0:T(8,128)(2,1)S(1)}, bf16[512,128]{1,0:T(8,128)(2,1)S(1)}, bf16[512,128]{1,0:T(8,128)(2...) custom-call(s32[65]{0:T(128)S(1)} %copy-done.6, ...), custom_call_target="tpu_custom_call" | custom-call | flops 67108864 | tf_op jit(solution)/shard_map/pallas_call | solution.py:552
  35.6 2.5 %collective-permute-start.9 = (bf16[512,128]{1,0:T(8,128)(2,1)S(1)}, bf16[512,128]{1,0:T(8,128)(2,1)S(1)}, u32[]{:S(2)}, u32[]{:S(2)}) collective-permute-start(bf16[512,128]{1,0:T(8,128)(2,1)S(1)} %get-tuple-element.80), channel_id=1, source_target_pairs={{0,24},{4,28},{8,16},{12,20},{16,8},{20,12},{24,0},{28,4},{1,25},{... | collective-permute-start | bytes 393224 | tf_op jit(solution)/shard_map/ppermute | solution.py:443
  38.1 2.0 %collective-permute-start.10 = (bf16[512,128]{1,0:T(8,128)(2,1)S(1)}, bf16[512,128]{1,0:T(8,128)(2,1)S(1)}, u32[]{:S(2)}, u32[]{:S(2)}) collective-permute-start(bf16[512,128]{1,0:T(8,128)(2,1)S(1)} %get-tuple-element.81), channel_id=1, source_target_pairs={{0,28},{4,24},{8,20},{12,16},{16,12},{20,8},{24,4},{28,0},{1,29},{... | collective-permute-start | bytes 393224 | tf_op jit(solution)/shard_map/ppermute | solution.py:443
  40.1 2.3 %collective-permute-start.12 = (bf16[512,128]{1,0:T(8,128)(2,1)S(1)}, bf16[512,128]{1,0:T(8,128)(2,1)S(1)}, u32[]{:S(2)}, u32[]{:S(2)}) collective-permute-start(bf16[512,128]{1,0:T(8,128)(2,1)S(1)} %get-tuple-element.83), channel_id=1, source_target_pairs={{0,12},{4,8},{8,4},{12,0},{16,28},{20,24},{24,20},{28,16},{1,13},{... | collective-permute-start | bytes 393224 | tf_op jit(solution)/shard_map/ppermute | solution.py:443
  42.4 1.2 collective-permute-start.13
  43.6 1.1 collective-permute-start.7
  44.7 2.4 %collective-permute-done.10.refs_1_.refs_7_ = bf16[512,128]{1,0:T(8,128)(2,1)S(1)} collective-permute-done((bf16[512,128]{1,0:T(8,128)(2,1)S(1)}, bf16[512,128]{1,0:T(8,128)(2,1)S(1)}, u32[]{:S(2)}, u32[]{:S(2)}) %collective-permute-start.10) | collective-permute-done | bytes 131104 | tf_op jit(solution)/shard_map/ppermute | solution.py:443
  47.1 2.2 %collective-permute-start.8 = (bf16[512,128]{1,0:T(8,128)(2,1)S(1)}, bf16[512,128]{1,0:T(8,128)(2,1)S(1)}, u32[]{:S(2)}, u32[]{:S(2)}) collective-permute-start(bf16[512,128]{1,0:T(8,128)(2,1)S(1)} %get-tuple-element.79), channel_id=1, source_target_pairs={{0,20},{4,16},{8,28},{12,24},{16,4},{20,0},{24,12},{28,8},{1,21},{... | collective-permute-start | bytes 393224 | tf_op jit(solution)/shard_map/ppermute | solution.py:443
  49.4 1.9 %collective-permute-done.11.refs_2_ = bf16[512,128]{1,0:T(8,128)(2,1)S(1)} collective-permute-done((bf16[512,128]{1,0:T(8,128)(2,1)S(1)}, bf16[512,128]{1,0:T(8,128)(2,1)S(1)}, u32[]{:S(2)}, u32[]{:S(2)}) %collective-permute-start.11) | collective-permute-done | bytes 131104 | tf_op jit(solution)/shard_map/ppermute | solution.py:443
  51.3 4.2 %collective-permute-done.12.refs_3_ = bf16[512,128]{1,0:T(8,128)(2,1)S(1)} collective-permute-done((bf16[512,128]{1,0:T(8,128)(2,1)S(1)}, bf16[512,128]{1,0:T(8,128)(2,1)S(1)}, u32[]{:S(2)}, u32[]{:S(2)}) %collective-permute-start.12) | collective-permute-done | bytes 131104 | tf_op jit(solution)/shard_map/ppermute | solution.py:443
  55.4 2.6 %shard_map.107 = (f32[2048,512]{1,0:T(8,128)S(1)}, f32[2,8,256]{2,1,0:T(8,128)S(1)}) custom-call(s32[65]{0:T(128)S(1)} %copy-done.6, s32[8]{0:T(128)S(1)} %copy-done.3, f32[4,256,128]{2,1,0:T(8,128)S(1)} %get-tuple-element.67.side_ref, f32[1,512]{1,0:T(1,128)S(1)} %bitcast.1, bf16[2048,512]{1,0:T(8,128)(2,1)S(1)} %get-tuple-element.66.q_ref, ...), custom_call_target="tpu_custom_call" | custom-call | flops 134217728 | tf_op jit(solution)/shard_map/pallas_call | solution.py:567
  58.0 0.6 collective-permute-done.8.refs_1_.refs_5_
  58.6 1.4 %shard_map.108 = (f32[2048,512]{1,0:T(8,128)S(1)}, f32[2,8,256]{2,1,0:T(8,128)S(1)}) custom-call(s32[65]{0:T(128)S(1)} %copy-done.6, s32[8]{0:T(128)S(1)} %copy-done.3, f32[4,256,128]{2,1,0:T(8,128)S(1)} %get-tuple-element.67.side_ref, f32[1,512]{1,0:T(1,128)S(1)} %bitcast.2, ...), custom_call_target="tpu_custom_call", output_to_operand_aliasing={{0}: (10, {})} | custom-call | flops 134217728 | tf_op jit(solution)/shard_map/pallas_call | solution.py:567
  60.1 1.6 %collective-permute-start.15 = (f32[2,8,256]{2,1,0:T(8,128)S(1)}, f32[2,8,256]{2,1,0:T(8,128)S(1)}, u32[]{:S(2)}, u32[]{:S(2)}) collective-permute-start(f32[2,8,256]{2,1,0:T(8,128)S(1)} %get-tuple-element.89.refs_3_), channel_id=1, source_target_pairs={{0,2},{1,3},{2,0},{3,1},{4,6},{5,7},{6,4},{7,5},{8,10},{9,11},{10,... | collective-permute-start | bytes 49160 | tf_op jit(solution)/shard_map/ppermute | solution.py:443
  61.9 2.0 %collective-permute-done.15.refs_1_ = f32[2,8,256]{2,1,0:T(8,128)S(1)} collective-permute-done((f32[2,8,256]{2,1,0:T(8,128)S(1)}, f32[2,8,256]{2,1,0:T(8,128)S(1)}, u32[]{:S(2)}, u32[]{:S(2)}) %collective-permute-start.15) | collective-permute-done | bytes 16416 | tf_op jit(solution)/shard_map/ppermute | solution.py:443
  63.9 0.9 collective-permute-done.14.refs_0_
  64.8 1.7 %shard_map.109 = (bf16[2048,512]{1,0:T(8,128)(2,1)S(1)}, bf16[512,128]{1,0:T(8,128)(2,1)S(1)}, bf16[512,128]{1,0:T(8,128)(2,1)S(1)}) custom-call(s32[65]{0:T(128)S(1)} %copy-done.6, s32[8]{0:T(128)S(1)} %copy-done.3, f32[4,256,128]{2,1,0:T(8,128)S(1)} %get-tuple-element.67.side_ref, f32[1,512]{1,0:T(1,128)S(1)} %bitcast.3, ...), custom_call_target="tpu_custom_call" | custom-call | flops 134217728 | tf_op jit(solution)/shard_map/pallas_call | solution.py:584
  66.5 2.8 %shard_map.110 = (bf16[2048,512]{1,0:T(8,128)(2,1)S(1)}, bf16[512,128]{1,0:T(8,128)(2,1)S(1)}, bf16[512,128]{1,0:T(8,128)(2,1)S(1)}, bf16[512,128]{1,0:T(8,128)(...) custom-call(s32[65]{0:T(128)S(1)} %copy-done.6, ...), custom_call_target="tpu_custom_call", output_to_operand_aliasing={{0}: (11, {})} | custom-call | flops 134217728 | tf_op jit(solution)/shard_map/pallas_call | solution.py:584
  69.3 1.4 %collective-permute-start.17 = (bf16[512,128]{1,0:T(8,128)(2,1)S(1)}, bf16[512,128]{1,0:T(8,128)(2,1)S(1)}, u32[]{:S(2)}, u32[]{:S(2)}) collective-permute-start(bf16[512,128]{1,0:T(8,128)(2,1)S(1)} %get-tuple-element.100), channel_id=1, source_target_pairs={{0,4},{4,0},{8,12},{12,8},{16,20},{20,16},{24,28},{28,24},{1,5},{5... | collective-permute-start | bytes 393224 | tf_op jit(solution)/shard_map/ppermute | solution.py:443
  70.7 2.2 %collective-permute-start.19 = (bf16[512,128]{1,0:T(8,128)(2,1)S(1)}, bf16[512,128]{1,0:T(8,128)(2,1)S(1)}, u32[]{:S(2)}, u32[]{:S(2)}) collective-permute-start(bf16[512,128]{1,0:T(8,128)(2,1)S(1)} %get-tuple-element.102), channel_id=1, source_target_pairs={{0,12},{4,8},{8,4},{12,0},{16,28},{20,24},{24,20},{28,16},{1,13},{... | collective-permute-start | bytes 393224 | tf_op jit(solution)/shard_map/ppermute | solution.py:443
  73.3 3.2 %collective-permute-start.21 = (bf16[512,128]{1,0:T(8,128)(2,1)S(1)}, bf16[512,128]{1,0:T(8,128)(2,1)S(1)}, u32[]{:S(2)}, u32[]{:S(2)}) collective-permute-start(bf16[512,128]{1,0:T(8,128)(2,1)S(1)} %get-tuple-element.104), channel_id=1, source_target_pairs={{0,20},{4,16},{8,28},{12,24},{16,4},{20,0},{24,12},{28,8},{1,21},{... | collective-permute-start | bytes 393224 | tf_op jit(solution)/shard_map/ppermute | solution.py:443
  76.5 1.5 %collective-permute-start.22 = (bf16[512,128]{1,0:T(8,128)(2,1)S(1)}, bf16[512,128]{1,0:T(8,128)(2,1)S(1)}, u32[]{:S(2)}, u32[]{:S(2)}) collective-permute-start(bf16[512,128]{1,0:T(8,128)(2,1)S(1)} %get-tuple-element.105), channel_id=1, source_target_pairs={{0,24},{4,28},{8,16},{12,20},{16,8},{20,12},{24,0},{28,4},{1,25},{... | collective-permute-start | bytes 393224 | tf_op jit(solution)/shard_map/ppermute | solution.py:443
  78.0 1.9 %collective-permute-done.18.refs_2_ = bf16[512,128]{1,0:T(8,128)(2,1)S(1)} collective-permute-done((bf16[512,128]{1,0:T(8,128)(2,1)S(1)}, bf16[512,128]{1,0:T(8,128)(2,1)S(1)}, u32[]{:S(2)}, u32[]{:S(2)}) %collective-permute-start.18) | collective-permute-done | bytes 131104 | tf_op jit(solution)/shard_map/ppermute | solution.py:443
  79.9 2.3 %collective-permute-start.23 = (bf16[512,128]{1,0:T(8,128)(2,1)S(1)}, bf16[512,128]{1,0:T(8,128)(2,1)S(1)}, u32[]{:S(2)}, u32[]{:S(2)}) collective-permute-start(bf16[512,128]{1,0:T(8,128)(2,1)S(1)} %get-tuple-element.106), channel_id=1, source_target_pairs={{0,28},{4,24},{8,20},{12,16},{16,12},{20,8},{24,4},{28,0},{1,29},{... | collective-permute-start | bytes 393224 | tf_op jit(solution)/shard_map/ppermute | solution.py:443
  82.3 9.1 %collective-permute-done.20.refs_4_ = bf16[512,128]{1,0:T(8,128)(2,1)S(1)} collective-permute-done((bf16[512,128]{1,0:T(8,128)(2,1)S(1)}, bf16[512,128]{1,0:T(8,128)(2,1)S(1)}, u32[]{:S(2)}, u32[]{:S(2)}) %collective-permute-start.20) | collective-permute-done | bytes 131104 | tf_op jit(solution)/shard_map/ppermute | solution.py:443
  91.4 3.5 %collective-permute-done.21.refs_5_ = bf16[512,128]{1,0:T(8,128)(2,1)S(1)} collective-permute-done((bf16[512,128]{1,0:T(8,128)(2,1)S(1)}, bf16[512,128]{1,0:T(8,128)(2,1)S(1)}, u32[]{:S(2)}, u32[]{:S(2)}) %collective-permute-start.21) | collective-permute-done | bytes 131104 | tf_op jit(solution)/shard_map/ppermute | solution.py:443
  94.9 1.2 shard_map.113
  96.2 1.6 %collective-permute-start.26 = (bf16[512,128]{1,0:T(8,128)(2,1)S(1)}, bf16[512,128]{1,0:T(8,128)(2,1)S(1)}, u32[]{:S(2)}, u32[]{:S(2)}) collective-permute-start(bf16[512,128]{1,0:T(8,128)(2,1)S(1)} %get-tuple-element.109), channel_id=1, source_target_pairs={{0,24},{4,28},{8,16},{12,20},{16,8},{20,12},{24,0},{28,4},{1,25},{... | collective-permute-start | bytes 393224 | tf_op jit(solution)/shard_map/ppermute | solution.py:443
  97.7 2.5 %collective-permute-start.27 = (bf16[512,128]{1,0:T(8,128)(2,1)S(1)}, bf16[512,128]{1,0:T(8,128)(2,1)S(1)}, u32[]{:S(2)}, u32[]{:S(2)}) collective-permute-start(bf16[512,128]{1,0:T(8,128)(2,1)S(1)} %get-tuple-element.110), channel_id=1, source_target_pairs={{0,28},{4,24},{8,20},{12,16},{16,12},{20,8},{24,4},{28,0},{1,29},{... | collective-permute-start | bytes 393224 | tf_op jit(solution)/shard_map/ppermute | solution.py:443
  100.2 6.8 %shard_map.111 = (bf16[2048,512]{1,0:T(8,128)(2,1)}, f32[1024,512]{1,0:T(8,128)S(1)}, f32[1024,512]{1,0:T(8,128)S(1)}) custom-call(s32[65]{0:T(128)S(1)} %copy-done.6, s32[8]{0:T(128)S(1)} %copy-done.3, f32[4]{0:T(128)S(1)} %copy-done.4, f32[8,256]{1,0:T(8,128)S(1)} %get-tuple-element.65.refs_8_.seg_ref, bf16[2048,512]{1,0:T(8,128)(2,1)S(1)} %get-tuple-element.66.q_ref, ...), custom_call_target="tpu_custom_call" | custom-call | flops 1610612736 | tf_op jit(solution)/shard_map/pallas_call | solution.py:603
  107.1 7.8 %collective-permute-start.24 = (bf16[512,128]{1,0:T(8,128)(2,1)S(1)}, bf16[512,128]{1,0:T(8,128)(2,1)S(1)}, u32[]{:S(2)}, u32[]{:S(2)}) collective-permute-start(bf16[512,128]{1,0:T(8,128)(2,1)S(1)} %get-tuple-element.107), channel_id=1, source_target_pairs={{0,16},{4,20},{8,24},{12,28},{16,0},{20,4},{24,8},{28,12},{1,17},{... | collective-permute-start | bytes 393224 | tf_op jit(solution)/shard_map/ppermute | solution.py:443
  115.0 3.3 %collective-permute-start.28 = (bf16[512,128]{1,0:T(8,128)(2,1)S(1)}, bf16[512,128]{1,0:T(8,128)(2,1)S(1)}, u32[]{:S(2)}, u32[]{:S(2)}) collective-permute-start(bf16[512,128]{1,0:T(8,128)(2,1)S(1)} %get-tuple-element.111), channel_id=1, source_target_pairs={{0,8},{4,12},{8,0},{12,4},{16,24},{20,28},{24,16},{28,20},{1,9},{5... | collective-permute-start | bytes 393224 | tf_op jit(solution)/shard_map/ppermute | solution.py:443
  118.3 1.5 %collective-permute-start.30 = (bf16[512,128]{1,0:T(8,128)(2,1)S(1)}, bf16[512,128]{1,0:T(8,128)(2,1)S(1)}, u32[]{:S(2)}, u32[]{:S(2)}) collective-permute-start(bf16[512,128]{1,0:T(8,128)(2,1)S(1)} %get-tuple-element.114), channel_id=1, source_target_pairs={{0,4},{4,0},{8,12},{12,8},{16,20},{20,16},{24,28},{28,24},{1,5},{5... | collective-permute-start | bytes 393224 | tf_op jit(solution)/shard_map/ppermute | solution.py:443
  119.8 6.8 %shard_map.112 = (bf16[2048,512]{1,0:T(8,128)(2,1)}, f32[1024,512]{1,0:T(8,128)S(1)}, f32[1024,512]{1,0:T(8,128)S(1)}) custom-call(s32[65]{0:T(128)S(1)} %copy-done.6, s32[8]{0:T(128)S(1)} %copy-done.3, f32[4]{0:T(128)S(1)} %copy-done.4, f32[8,256]{1,0:T(8,128)S(1)} %get-tuple-element.65.refs_8_.seg_ref, ...), custom_call_target="tpu_custom_call", output_to_operand_aliasing={{0}: (16, {})} | custom-call | flops 1610612736 | tf_op jit(solution)/shard_map/pallas_call | solution.py:603
  126.7 3.8 %shard_map.114 = (bf16[2048,512]{1,0:T(8,128)(2,1)}, bf16[2048,512]{1,0:T(8,128)(2,1)}) custom-call(s32[65]{0:T(128)S(1)} %copy-done.7, s32[8]{0:T(128)S(1)} %copy-done.3, f32[4]{0:T(128)S(1)} %copy-done.4, bf16[2048,512]{1,0:T(8,128)(2,1)S(1)} %get-tuple-element.63.k_ref, bf16[2048,512]{1,0:T(8,128)(2,1)S(1)} %get-tuple-element.64.v_ref, ...), custom_call_target="tpu_custom_call" | custom-call | flops 268435456 | tf_op jit(solution)/shard_map/pallas_call | solution.py:620
  130.5 2.1 %shard_map.115 = (bf16[2048,512]{1,0:T(8,128)(2,1)}, bf16[2048,512]{1,0:T(8,128)(2,1)}) custom-call(s32[65]{0:T(128)S(1)} %copy-done.7, s32[8]{0:T(128)S(1)} %copy-done.3, f32[4]{0:T(128)S(1)} %copy-done.4, bf16[2048,512]{1,0:T(8,128)(2,1)S(1)} %get-tuple-element.63.k_ref, ...), custom_call_target="tpu_custom_call", output_to_operand_aliasing={{0}: (11, {}), {1}: (12, {})} | custom-call | flops 268435456 | tf_op jit(solution)/shard_map/pallas_call | solution.py:620
  (45 shorter events, 1.4 us)
Async XLA Ops:
  3.8 14.4 %collective-permute-start.5 = (bf16[528,128]{1,0:T(8,128)(2,1)}, bf16[528,128]{1,0:T(8,128)(2,1)S(1)}, u32[]{:S(2)}, u32[]{:S(2)}) collective-permute-start(bf16[528,128]{1,0:T(8,128)(2,1)} %get-tuple-element.76), channel_id=1, source_target_pairs={{0,24},{4,28},{8,16},{12,20},{16,8},{20,12},{24,0},{28,4},{1,25},{... | collective-permute-start | bytes 405512 | tf_op jit(solution)/shard_map/ppermute | solution.py:443
  9.0 11.5 %collective-permute-start.6 = (bf16[528,128]{1,0:T(8,128)(2,1)}, bf16[528,128]{1,0:T(8,128)(2,1)S(1)}, u32[]{:S(2)}, u32[]{:S(2)}) collective-permute-start(bf16[528,128]{1,0:T(8,128)(2,1)} %get-tuple-element.77), channel_id=1, source_target_pairs={{0,28},{4,24},{8,20},{12,16},{16,12},{20,8},{24,4},{28,0},{1,29},{... | collective-permute-start | bytes 405512 | tf_op jit(solution)/shard_map/ppermute | solution.py:443
  10.2 13.2 %copy-start.3 = (s32[8]{0:T(128)S(1)}, s32[8]{0:T(128)}, u32[]{:S(2)}) copy-start(s32[8]{0:T(128)} %home_ref.17) | copy-start | bytes 100
  10.2 13.2 %copy-start.4 = (f32[4]{0:T(128)S(1)}, f32[4]{0:T(128)}, u32[]{:S(2)}) copy-start(f32[4]{0:T(128)} %rate_ref.13) | copy-start | bytes 52
  10.2 13.2 %copy-start.8 = (s32[32]{0:T(128)S(1)}, s32[32]{0:T(128)}, u32[]{:S(2)}) copy-start(s32[32]{0:T(128)} %len_ref.1) | copy-start | bytes 388
  14.7 16.2 %collective-permute-start = (bf16[528,128]{1,0:T(8,128)(2,1)}, bf16[528,128]{1,0:T(8,128)(2,1)S(1)}, u32[]{:S(2)}, u32[]{:S(2)}) collective-permute-start(bf16[528,128]{1,0:T(8,128)(2,1)} %get-tuple-element.71), channel_id=1, source_target_pairs={{0,4},{4,0},{8,12},{12,8},{16,20},{20,16},{24,28},{28,24},{1,5},{5... | collective-permute-start | bytes 405512 | tf_op jit(solution)/shard_map/ppermute | solution.py:443
  15.1 15.8 %collective-permute-start.1 = (bf16[528,128]{1,0:T(8,128)(2,1)}, bf16[528,128]{1,0:T(8,128)(2,1)S(1)}, u32[]{:S(2)}, u32[]{:S(2)}) collective-permute-start(bf16[528,128]{1,0:T(8,128)(2,1)} %get-tuple-element.72), channel_id=1, source_target_pairs={{0,8},{4,12},{8,0},{12,4},{16,24},{20,28},{24,16},{28,20},{1,9},{5... | collective-permute-start | bytes 405512 | tf_op jit(solution)/shard_map/ppermute | solution.py:443
  15.1 15.8 %collective-permute-start.2 = (bf16[528,128]{1,0:T(8,128)(2,1)}, bf16[528,128]{1,0:T(8,128)(2,1)S(1)}, u32[]{:S(2)}, u32[]{:S(2)}) collective-permute-start(bf16[528,128]{1,0:T(8,128)(2,1)} %get-tuple-element.73), channel_id=1, source_target_pairs={{0,12},{4,8},{8,4},{12,0},{16,28},{20,24},{24,20},{28,16},{1,13},{... | collective-permute-start | bytes 405512 | tf_op jit(solution)/shard_map/ppermute | solution.py:443
  18.3 13.1 %collective-permute-start.3 = (bf16[528,128]{1,0:T(8,128)(2,1)}, bf16[528,128]{1,0:T(8,128)(2,1)S(1)}, u32[]{:S(2)}, u32[]{:S(2)}) collective-permute-start(bf16[528,128]{1,0:T(8,128)(2,1)} %get-tuple-element.74), channel_id=1, source_target_pairs={{0,16},{4,20},{8,24},{12,28},{16,0},{20,4},{24,8},{28,12},{1,17},{... | collective-permute-start | bytes 405512 | tf_op jit(solution)/shard_map/ppermute | solution.py:443
  20.5 12.9 %collective-permute-start.4 = (bf16[528,128]{1,0:T(8,128)(2,1)}, bf16[528,128]{1,0:T(8,128)(2,1)S(1)}, u32[]{:S(2)}, u32[]{:S(2)}) collective-permute-start(bf16[528,128]{1,0:T(8,128)(2,1)} %get-tuple-element.75), channel_id=1, source_target_pairs={{0,20},{4,16},{8,28},{12,24},{16,4},{20,0},{24,12},{28,8},{1,21},{... | collective-permute-start | bytes 405512 | tf_op jit(solution)/shard_map/ppermute | solution.py:443
  23.3 1.6 %copy-start = (bf16[2048,512]{1,0:T(8,128)(2,1)S(1)}, bf16[2048,512]{1,0:T(8,128)(2,1)}, u32[]{:S(2)}) copy-start(bf16[2048,512]{1,0:T(8,128)(2,1)} %q_hbm.1) | copy-start | bytes 6291460
  24.9 1.6 %copy-start.1 = (bf16[2048,512]{1,0:T(8,128)(2,1)S(1)}, bf16[2048,512]{1,0:T(8,128)(2,1)}, u32[]{:S(2)}) copy-start(bf16[2048,512]{1,0:T(8,128)(2,1)} %u_hbm.1) | copy-start | bytes 6291460
  26.5 6.8 %copy-start.2 = (bf16[528,128]{1,0:T(8,128)(2,1)S(1)}, bf16[528,128]{1,0:T(8,128)(2,1)}, u32[]{:S(2)}) copy-start(bf16[528,128]{1,0:T(8,128)(2,1)} %get-tuple-element.70.refs_0_) | copy-start | bytes 405508
  26.5 6.8 %copy-start.6 = (s32[65]{0:T(128)S(1)}, s32[65]{0:T(128)}, u32[]{:S(2)}) copy-start(s32[65]{0:T(128)} %get-tuple-element.61.first_ref) | copy-start | bytes 784
  26.5 28.9 %copy-start.5 = (f32[512]{0:T(512)S(1)}, f32[512]{0:T(512)}, u32[]{:S(2)}) copy-start(f32[512]{0:T(512)} %param.12) | copy-start | bytes 6148
  35.6 8.0 %collective-permute-start.9 = (bf16[512,128]{1,0:T(8,128)(2,1)S(1)}, bf16[512,128]{1,0:T(8,128)(2,1)S(1)}, u32[]{:S(2)}, u32[]{:S(2)}) collective-permute-start(bf16[512,128]{1,0:T(8,128)(2,1)S(1)} %get-tuple-element.80), channel_id=1, source_target_pairs={{0,24},{4,28},{8,16},{12,20},{16,8},{20,12},{24,0},{28,4},{1,25},{... | collective-permute-start | bytes 393224 | tf_op jit(solution)/shard_map/ppermute | solution.py:443
  38.1 9.1 %collective-permute-start.10 = (bf16[512,128]{1,0:T(8,128)(2,1)S(1)}, bf16[512,128]{1,0:T(8,128)(2,1)S(1)}, u32[]{:S(2)}, u32[]{:S(2)}) collective-permute-start(bf16[512,128]{1,0:T(8,128)(2,1)S(1)} %get-tuple-element.81), channel_id=1, source_target_pairs={{0,28},{4,24},{8,20},{12,16},{16,12},{20,8},{24,4},{28,0},{1,29},{... | collective-permute-start | bytes 393224 | tf_op jit(solution)/shard_map/ppermute | solution.py:443
  40.1 11.2 %collective-permute-start.11 = (bf16[512,128]{1,0:T(8,128)(2,1)S(1)}, bf16[512,128]{1,0:T(8,128)(2,1)S(1)}, u32[]{:S(2)}, u32[]{:S(2)}) collective-permute-start(bf16[512,128]{1,0:T(8,128)(2,1)S(1)} %get-tuple-element.82), channel_id=1, source_target_pairs={{0,8},{4,12},{8,0},{12,4},{16,24},{20,28},{24,16},{28,20},{1,9},{5... | collective-permute-start | bytes 393224 | tf_op jit(solution)/shard_map/ppermute | solution.py:443
  40.1 15.3 %collective-permute-start.12 = (bf16[512,128]{1,0:T(8,128)(2,1)S(1)}, bf16[512,128]{1,0:T(8,128)(2,1)S(1)}, u32[]{:S(2)}, u32[]{:S(2)}) collective-permute-start(bf16[512,128]{1,0:T(8,128)(2,1)S(1)} %get-tuple-element.83), channel_id=1, source_target_pairs={{0,12},{4,8},{8,4},{12,0},{16,28},{20,24},{24,20},{28,16},{1,13},{... | collective-permute-start | bytes 393224 | tf_op jit(solution)/shard_map/ppermute | solution.py:443
  42.4 13.1 %collective-permute-start.13 = (bf16[512,128]{1,0:T(8,128)(2,1)S(1)}, bf16[512,128]{1,0:T(8,128)(2,1)S(1)}, u32[]{:S(2)}, u32[]{:S(2)}) collective-permute-start(bf16[512,128]{1,0:T(8,128)(2,1)S(1)} %get-tuple-element.85), channel_id=1, source_target_pairs={{0,4},{4,0},{8,12},{12,8},{16,20},{20,16},{24,28},{28,24},{1,5},{5... | collective-permute-start | bytes 393224 | tf_op jit(solution)/shard_map/ppermute | solution.py:443
  43.6 14.4 %collective-permute-start.7 = (bf16[512,128]{1,0:T(8,128)(2,1)S(1)}, bf16[512,128]{1,0:T(8,128)(2,1)S(1)}, u32[]{:S(2)}, u32[]{:S(2)}) collective-permute-start(bf16[512,128]{1,0:T(8,128)(2,1)S(1)} %get-tuple-element.78), channel_id=1, source_target_pairs={{0,16},{4,20},{8,24},{12,28},{16,0},{20,4},{24,8},{28,12},{1,17},{... | collective-permute-start | bytes 393224 | tf_op jit(solution)/shard_map/ppermute | solution.py:443
  47.1 11.5 %collective-permute-start.8 = (bf16[512,128]{1,0:T(8,128)(2,1)S(1)}, bf16[512,128]{1,0:T(8,128)(2,1)S(1)}, u32[]{:S(2)}, u32[]{:S(2)}) collective-permute-start(bf16[512,128]{1,0:T(8,128)(2,1)S(1)} %get-tuple-element.79), channel_id=1, source_target_pairs={{0,20},{4,16},{8,28},{12,24},{16,4},{20,0},{24,12},{28,8},{1,21},{... | collective-permute-start | bytes 393224 | tf_op jit(solution)/shard_map/ppermute | solution.py:443
  60.0 1.9 %collective-permute-start.16 = (f32[2,8,256]{2,1,0:T(8,128)S(1)}, f32[2,8,256]{2,1,0:T(8,128)S(1)}, u32[]{:S(2)}, u32[]{:S(2)}) collective-permute-start(f32[2,8,256]{2,1,0:T(8,128)S(1)} %get-tuple-element.89.refs_3_), channel_id=1, source_target_pairs={{0,1},{1,0},{2,3},{3,2},{4,5},{5,4},{6,7},{7,6},{8,9},{9,8},{10,11... | collective-permute-start | bytes 49160 | tf_op jit(solution)/shard_map/ppermute | solution.py:443
  60.1 3.8 %collective-permute-start.15 = (f32[2,8,256]{2,1,0:T(8,128)S(1)}, f32[2,8,256]{2,1,0:T(8,128)S(1)}, u32[]{:S(2)}, u32[]{:S(2)}) collective-permute-start(f32[2,8,256]{2,1,0:T(8,128)S(1)} %get-tuple-element.89.refs_3_), channel_id=1, source_target_pairs={{0,2},{1,3},{2,0},{3,1},{4,6},{5,7},{6,4},{7,5},{8,10},{9,11},{10,... | collective-permute-start | bytes 49160 | tf_op jit(solution)/shard_map/ppermute | solution.py:443
  61.7 3.2 %collective-permute-start.14 = (f32[2,8,256]{2,1,0:T(8,128)S(1)}, f32[2,8,256]{2,1,0:T(8,128)S(1)}, u32[]{:S(2)}, u32[]{:S(2)}) collective-permute-start(f32[2,8,256]{2,1,0:T(8,128)S(1)} %get-tuple-element.89.refs_3_), channel_id=1, source_target_pairs={{0,3},{1,2},{2,1},{3,0},{4,7},{5,6},{6,5},{7,4},{8,11},{9,10},{10,... | collective-permute-start | bytes 49160 | tf_op jit(solution)/shard_map/ppermute | solution.py:443
  69.3 7.2 %collective-permute-start.17 = (bf16[512,128]{1,0:T(8,128)(2,1)S(1)}, bf16[512,128]{1,0:T(8,128)(2,1)S(1)}, u32[]{:S(2)}, u32[]{:S(2)}) collective-permute-start(bf16[512,128]{1,0:T(8,128)(2,1)S(1)} %get-tuple-element.100), channel_id=1, source_target_pairs={{0,4},{4,0},{8,12},{12,8},{16,20},{20,16},{24,28},{28,24},{1,5},{5... | collective-permute-start | bytes 393224 | tf_op jit(solution)/shard_map/ppermute | solution.py:443
  70.7 9.3 %collective-permute-start.18 = (bf16[512,128]{1,0:T(8,128)(2,1)S(1)}, bf16[512,128]{1,0:T(8,128)(2,1)S(1)}, u32[]{:S(2)}, u32[]{:S(2)}) collective-permute-start(bf16[512,128]{1,0:T(8,128)(2,1)S(1)} %get-tuple-element.101), channel_id=1, source_target_pairs={{0,8},{4,12},{8,0},{12,4},{16,24},{20,28},{24,16},{28,20},{1,9},{5... | collective-permute-start | bytes 393224 | tf_op jit(solution)/shard_map/ppermute | solution.py:443
  70.7 11.6 %collective-permute-start.19 = (bf16[512,128]{1,0:T(8,128)(2,1)S(1)}, bf16[512,128]{1,0:T(8,128)(2,1)S(1)}, u32[]{:S(2)}, u32[]{:S(2)}) collective-permute-start(bf16[512,128]{1,0:T(8,128)(2,1)S(1)} %get-tuple-element.102), channel_id=1, source_target_pairs={{0,12},{4,8},{8,4},{12,0},{16,28},{20,24},{24,20},{28,16},{1,13},{... | collective-permute-start | bytes 393224 | tf_op jit(solution)/shard_map/ppermute | solution.py:443
  72.9 18.5 %collective-permute-start.20 = (bf16[512,128]{1,0:T(8,128)(2,1)S(1)}, bf16[512,128]{1,0:T(8,128)(2,1)S(1)}, u32[]{:S(2)}, u32[]{:S(2)}) collective-permute-start(bf16[512,128]{1,0:T(8,128)(2,1)S(1)} %get-tuple-element.103), channel_id=1, source_target_pairs={{0,16},{4,20},{8,24},{12,28},{16,0},{20,4},{24,8},{28,12},{1,17},{... | collective-permute-start | bytes 393224 | tf_op jit(solution)/shard_map/ppermute | solution.py:443
  73.3 21.6 %collective-permute-start.21 = (bf16[512,128]{1,0:T(8,128)(2,1)S(1)}, bf16[512,128]{1,0:T(8,128)(2,1)S(1)}, u32[]{:S(2)}, u32[]{:S(2)}) collective-permute-start(bf16[512,128]{1,0:T(8,128)(2,1)S(1)} %get-tuple-element.104), channel_id=1, source_target_pairs={{0,20},{4,16},{8,28},{12,24},{16,4},{20,0},{24,12},{28,8},{1,21},{... | collective-permute-start | bytes 393224 | tf_op jit(solution)/shard_map/ppermute | solution.py:443
  76.5 18.4 %collective-permute-start.22 = (bf16[512,128]{1,0:T(8,128)(2,1)S(1)}, bf16[512,128]{1,0:T(8,128)(2,1)S(1)}, u32[]{:S(2)}, u32[]{:S(2)}) collective-permute-start(bf16[512,128]{1,0:T(8,128)(2,1)S(1)} %get-tuple-element.105), channel_id=1, source_target_pairs={{0,24},{4,28},{8,16},{12,20},{16,8},{20,12},{24,0},{28,4},{1,25},{... | collective-permute-start | bytes 393224 | tf_op jit(solution)/shard_map/ppermute | solution.py:443
  79.9 15.0 %collective-permute-start.23 = (bf16[512,128]{1,0:T(8,128)(2,1)S(1)}, bf16[512,128]{1,0:T(8,128)(2,1)S(1)}, u32[]{:S(2)}, u32[]{:S(2)}) collective-permute-start(bf16[512,128]{1,0:T(8,128)(2,1)S(1)} %get-tuple-element.106), channel_id=1, source_target_pairs={{0,28},{4,24},{8,20},{12,16},{16,12},{20,8},{24,4},{28,0},{1,29},{... | collective-permute-start | bytes 393224 | tf_op jit(solution)/shard_map/ppermute | solution.py:443
  96.2 22.1 %collective-permute-start.26 = (bf16[512,128]{1,0:T(8,128)(2,1)S(1)}, bf16[512,128]{1,0:T(8,128)(2,1)S(1)}, u32[]{:S(2)}, u32[]{:S(2)}) collective-permute-start(bf16[512,128]{1,0:T(8,128)(2,1)S(1)} %get-tuple-element.109), channel_id=1, source_target_pairs={{0,24},{4,28},{8,16},{12,20},{16,8},{20,12},{24,0},{28,4},{1,25},{... | collective-permute-start | bytes 393224 | tf_op jit(solution)/shard_map/ppermute | solution.py:443
  97.7 20.6 %collective-permute-start.27 = (bf16[512,128]{1,0:T(8,128)(2,1)S(1)}, bf16[512,128]{1,0:T(8,128)(2,1)S(1)}, u32[]{:S(2)}, u32[]{:S(2)}) collective-permute-start(bf16[512,128]{1,0:T(8,128)(2,1)S(1)} %get-tuple-element.110), channel_id=1, source_target_pairs={{0,28},{4,24},{8,20},{12,16},{16,12},{20,8},{24,4},{28,0},{1,29},{... | collective-permute-start | bytes 393224 | tf_op jit(solution)/shard_map/ppermute | solution.py:443
  107.1 23.4 %collective-permute-start.24 = (bf16[512,128]{1,0:T(8,128)(2,1)S(1)}, bf16[512,128]{1,0:T(8,128)(2,1)S(1)}, u32[]{:S(2)}, u32[]{:S(2)}) collective-permute-start(bf16[512,128]{1,0:T(8,128)(2,1)S(1)} %get-tuple-element.107), channel_id=1, source_target_pairs={{0,16},{4,20},{8,24},{12,28},{16,0},{20,4},{24,8},{28,12},{1,17},{... | collective-permute-start | bytes 393224 | tf_op jit(solution)/shard_map/ppermute | solution.py:443
  114.9 15.6 %collective-permute-start.25 = (bf16[512,128]{1,0:T(8,128)(2,1)S(1)}, bf16[512,128]{1,0:T(8,128)(2,1)S(1)}, u32[]{:S(2)}, u32[]{:S(2)}) collective-permute-start(bf16[512,128]{1,0:T(8,128)(2,1)S(1)} %get-tuple-element.108), channel_id=1, source_target_pairs={{0,20},{4,16},{8,28},{12,24},{16,4},{20,0},{24,12},{28,8},{1,21},{... | collective-permute-start | bytes 393224 | tf_op jit(solution)/shard_map/ppermute | solution.py:443
  115.0 11.7 %collective-permute-start.28 = (bf16[512,128]{1,0:T(8,128)(2,1)S(1)}, bf16[512,128]{1,0:T(8,128)(2,1)S(1)}, u32[]{:S(2)}, u32[]{:S(2)}) collective-permute-start(bf16[512,128]{1,0:T(8,128)(2,1)S(1)} %get-tuple-element.111), channel_id=1, source_target_pairs={{0,8},{4,12},{8,0},{12,4},{16,24},{20,28},{24,16},{28,20},{1,9},{5... | collective-permute-start | bytes 393224 | tf_op jit(solution)/shard_map/ppermute | solution.py:443
  118.3 8.3 %collective-permute-start.29 = (bf16[512,128]{1,0:T(8,128)(2,1)S(1)}, bf16[512,128]{1,0:T(8,128)(2,1)S(1)}, u32[]{:S(2)}, u32[]{:S(2)}) collective-permute-start(bf16[512,128]{1,0:T(8,128)(2,1)S(1)} %get-tuple-element.112), channel_id=1, source_target_pairs={{0,12},{4,8},{8,4},{12,0},{16,28},{20,24},{24,20},{28,16},{1,13},{... | collective-permute-start | bytes 393224 | tf_op jit(solution)/shard_map/ppermute | solution.py:443
  118.3 8.3 %collective-permute-start.30 = (bf16[512,128]{1,0:T(8,128)(2,1)S(1)}, bf16[512,128]{1,0:T(8,128)(2,1)S(1)}, u32[]{:S(2)}, u32[]{:S(2)}) collective-permute-start(bf16[512,128]{1,0:T(8,128)(2,1)S(1)} %get-tuple-element.114), channel_id=1, source_target_pairs={{0,4},{4,0},{8,12},{12,8},{16,20},{20,16},{24,28},{28,24},{1,5},{5... | collective-permute-start | bytes 393224 | tf_op jit(solution)/shard_map/ppermute | solution.py:443
  119.8 6.9 %copy-start.7 = (s32[65]{0:T(128)S(1)}, s32[65]{0:T(128)}, u32[]{:S(2)}) copy-start(s32[65]{0:T(128)} %get-tuple-element.62.refs_0_.last_ref) | copy-start | bytes 784
